TPU v7x, 256 devices: a whole 4x4x8 slice. The times are simulated.
256 devices in a mesh: hid: 128 (over x, z, y), seq: 2 (over core).
Axes of the slice: x: 4, y: 4, z: 8, core: 2. Of those that a mesh axis runs over, the one named last changes fastest.
Arguments:
- pre_act: bfloat16 [1536, 32768], P(('hid', 'seq')), may hold values from -6 to 6
- butterfly: bfloat16 [128, 5, 256, 256], P('hid'), may hold values from -0.15625 to 0.15625
- low_u: bfloat16 [32768, 256], P('hid'), may hold values from -0.25 to 0.25
- low_v: bfloat16 [256, 32768], P(None, 'hid'), may hold values from -0.0625 to 0.0625
- grad_out: bfloat16 [1536, 32768], P(('hid', 'seq')), may hold values from -6 to 6
Outputs:
- output: bfloat16 [1536, 32768], P(('hid', 'seq'))
- grad_pre: bfloat16 [1536, 32768], P(('hid', 'seq'))
- grad_butterfly: float32 [128, 5, 256, 256], P('hid', None, 'seq')
- grad_low_u: float32 [32768, 256], P('hid', 'seq')
- grad_low_v: float32 [256, 32768], P('seq', 'hid')
All inputs are finite; a program needn't handle non-finite values.
Results may differ from a plain program's by a relative error of at most 0.0075.
Values may be sent and summed in bfloat16 or wider, within the bound.
A program may use at most 64 MiB of HBM per device.

v0:
```python
import math

import jax
import jax.numpy as jnp
from jax import lax
from jax.sharding import PartitionSpec as P

LEVELS = 4


def swapped(x, axis, stride):
    return lax.ppermute(x, axis, [(i, i ^ 1 << stride) for i in range(lax.axis_size(axis))])


def gelu_tanh(value):
    return jax.nn.gelu(value, approximate=True)


def reduce_latent(partial_value):
    return lax.psum(partial_value, "hid").astype(jnp.bfloat16)


def inner_rows(left, right):
    return lax.dot_general(
        left, right, (((0,), (0,)), ((), ())), preferred_element_type=jnp.float32
    )


def on_device(pre_act, butterfly, low_u, low_v, grad_out):
    pre_f = pre_act.astype(jnp.float32)
    act_tok = gelu_tanh(pre_f).astype(jnp.bfloat16)
    act_rows = lax.all_to_all(act_tok, "hid", split_axis=1, concat_axis=0, tiled=True)
    partners = [act_rows]
    for level in range(LEVELS):
        partners.append(swapped(act_rows, "hid", level))
    latent = reduce_latent(jnp.dot(act_rows, low_u, preferred_element_type=jnp.float32))
    total = jnp.dot(latent, low_v, preferred_element_type=jnp.float32)
    for level in range(LEVELS + 1):
        total = total + jnp.dot(
            partners[level], butterfly[0, level], preferred_element_type=jnp.float32
        )
    output_rows = total.astype(jnp.bfloat16)
    output_tok = lax.all_to_all(output_rows, "hid", split_axis=0, concat_axis=1, tiled=True)
    grad_rows = lax.all_to_all(grad_out, "hid", split_axis=1, concat_axis=0, tiled=True)
    dlatent = reduce_latent(jnp.dot(grad_rows, low_v.T, preferred_element_type=jnp.float32))
    backward = jnp.dot(dlatent, low_u.T, preferred_element_type=jnp.float32)
    backward = backward + jnp.dot(grad_rows, butterfly[0, 0].T, preferred_element_type=jnp.float32)
    for level in range(1, LEVELS + 1):
        grad_far, weight_far = swapped((grad_rows, butterfly[0, level]), "hid", level - 1)
        backward = backward + jnp.dot(grad_far, weight_far.T, preferred_element_type=jnp.float32)
    grad_act = backward.astype(jnp.bfloat16)
    tokens_all = pre_act.shape[0] * lax.axis_size("hid") * lax.axis_size("seq")
    factor = 1.0 / math.sqrt(tokens_all)
    block_grads = jnp.stack(
        [inner_rows(partners[level], grad_rows) for level in range(LEVELS + 1)], axis=0
    )
    block_grads = block_grads[None] * factor
    low_u_grad = inner_rows(act_rows, dlatent) * factor
    low_v_grad = inner_rows(latent, grad_rows) * factor
    grad_butterfly, grad_low_u, grad_low_v = (
        lax.psum_scatter(
            block_grads.astype(jnp.bfloat16), "seq", scatter_dimension=2, tiled=True
        ).astype(jnp.float32),
        lax.psum_scatter(
            low_u_grad.astype(jnp.bfloat16), "seq", scatter_dimension=1, tiled=True
        ).astype(jnp.float32),
        lax.psum_scatter(
            low_v_grad.astype(jnp.bfloat16), "seq", scatter_dimension=0, tiled=True
        ).astype(jnp.float32),
    )
    grad_act_tok = lax.all_to_all(grad_act, "hid", split_axis=0, concat_axis=1, tiled=True)
    unused, pullback = jax.vjp(gelu_tanh, pre_f)
    grad_pre = pullback(grad_act_tok.astype(jnp.float32))[0].astype(jnp.bfloat16)
    return (output_tok, grad_pre, grad_butterfly, grad_low_u, grad_low_v)


def solution(mesh):
    in_specs = (
        P(("hid", "seq"), None),
        P("hid", None, None, None),
        P("hid", None),
        P(None, "hid"),
        P(("hid", "seq"), None),
    )
    out_specs = (
        P(("hid", "seq"), None),
        P(("hid", "seq"), None),
        P("hid", None, "seq", None),
        P("hid", "seq"),
        P("seq", "hid"),
    )
    return jax.shard_map(
        on_device, mesh=mesh, in_specs=in_specs, out_specs=out_specs, check_vma=False
    )
```

profile of v0, /device:TPU:2, one launch (start us, length us, event | category | flops | bytes accessed | tf_op | source)
XLA Modules:
  0.0 891.5 jit_solution(8323681859844052992)
XLA Ops:
  7.2 15.7 %all-to-all-start.2 = ((bf16[6,128,256]{2,0,1:T(8,128)(2,1)}), bf16[6,128,256]{2,0,1:T(8,128)(2,1)S(1)}, u32[]{:S(2)}, u32[]{:S(2)}) async-start(bf16[6,128,256]{2,0,1:T(8,128)(2,1)} %bitcast.95), calls=%async_computation.2 | async-start | bytes 1048576 | tf_op jit(solution)/shard_map/all_to_all | solution.py:44
  24.1 17.2 %all-to-all-done.2 = bf16[6,128,256]{2,0,1:T(8,128)(2,1)S(1)} async-done(((bf16[6,128,256]{2,0,1:T(8,128)(2,1)}), bf16[6,128,256]{2,0,1:T(8,128)(2,1)S(1)}, u32[]{:S(2)}, u32[]{:S(2)}) %all-to-all-start.2) | async-done | bytes 393248 | tf_op jit(solution)/shard_map/all_to_all | solution.py:44
  41.2 8.1 all-to-all-start
  50.1 3.0 collective-permute-start.7
  54.6 2.4 collective-permute-start.11
  58.6 10.2 %all-to-all-done = bf16[6,128,256]{2,0,1:T(8,128)(2,1)S(1)} async-done(((bf16[6,128,256]{2,0,1:T(8,128)(2,1)}), bf16[6,128,256]{2,0,1:T(8,128)(2,1)S(1)}, u32[]{:S(2)}, u32[]{:S(2)}) %all-to-all-start) | async-done | bytes 393248 | tf_op jit(solution)/shard_map/all_to_all | solution.py:32
  69.2 620.6 %all-reduce.2 = (bf16[768,256]{1,0:T(8,128)(2,1)}, bf16[768,256]{1,0:T(8,128)(2,1)}) all-reduce(f32[768,256]{1,0:T(8,128)S(1)} %fusion.41, f32[768,256]{1,0:T(8,128)S(1)} %fusion.42), channel_id=1, replica_groups=mesh['hid'=128,'seq'=2] {'hid'}, use_global_device_ids=true, to_apply=%region_0.0 | all-reduce | flops 393216 | bytes 2359296 | tf_op jit(solution)/shard_map/psum | solution.py:20
  691.5 2.1 convolution_add_fusion.1
  698.3 78.5 %reduce-scatter.10.cloned.1.call-done = bf16[128,256]{1,0:T(8,128)(2,1)} async-done(((bf16[256,256]{1,0:T(8,128)(2,1)}), bf16[128,256]{1,0:T(8,128)(2,1)}) %reduce-scatter.10.cloned.1.call-update) | async-done | bytes 65552
  778.4 15.6 %reduce-scatter.8.cloned.1.call-done = bf16[128,256]{1,0:T(8,128)(2,1)} async-done(((bf16[256,256]{1,0:T(8,128)(2,1)}), bf16[128,256]{1,0:T(8,128)(2,1)}) %reduce-scatter.8.cloned.1.call-update) | async-done | bytes 65552 | tf_op jit(solution)/shard_map/reduce_scatter | solution.py:67
  795.5 1.5 collective-permute-start.5
  797.0 2.5 collective-permute-start.10
  804.3 2.8 collective-permute-start.1
  807.1 10.3 %collective-permute-done.10 = bf16[768,256]{1,0:T(8,128)(2,1)S(1)} collective-permute-done((bf16[768,256]{1,0:T(8,128)(2,1)S(1)}, bf16[768,256]{1,0:T(8,128)(2,1)S(1)}, u32[]{:S(2)}, u32[]{:S(2)}) %collective-permute-start.10) | collective-permute-done | bytes 393248 | tf_op jit(solution)/shard_map/ppermute | solution.py:12
  819.2 3.5 collective-permute-start.3
  824.0 11.0 %all-to-all-start.3 = ((bf16[128,6,256]{2,1,0:T(8,128)(2,1)}), bf16[128,6,256]{2,1,0:T(8,128)(2,1)S(1)}, u32[]{:S(2)}, u32[]{:S(2)}) async-start(bf16[128,6,256]{2,1,0:T(8,128)(2,1)} %all_to_all.64), calls=%async_computation.3 | async-start | bytes 1048576 | tf_op jit(solution)/shard_map/all_to_all | solution.py:71
  835.0 2.0 fusion.12
  839.1 6.1 collective-permute-done.3
  846.2 2.3 multiply_convert_fusion
  851.6 5.6 all-to-all-done.3
  857.2 9.8 %all-to-all-start.1 = ((bf16[128,6,256]{2,1,0:T(8,128)(2,1)}), bf16[128,6,256]{2,1,0:T(8,128)(2,1)S(1)}, u32[]{:S(2)}, u32[]{:S(2)}) async-start(bf16[128,6,256]{2,1,0:T(8,128)(2,1)} %all_to_all.56), calls=%async_computation.1 | async-start | bytes 1048576 | tf_op jit(solution)/shard_map/all_to_all | solution.py:43
  867.2 1.5 fusion.18
  868.7 13.6 %all-to-all-done.1 = bf16[128,6,256]{2,1,0:T(8,128)(2,1)S(1)} async-done(((bf16[128,6,256]{2,1,0:T(8,128)(2,1)}), bf16[128,6,256]{2,1,0:T(8,128)(2,1)S(1)}, u32[]{:S(2)}, u32[]{:S(2)}) %all-to-all-start.1) | async-done | bytes 393248 | tf_op jit(solution)/shard_map/all_to_all | solution.py:43
  882.3 1.9 convert_element_type.67
  (79 shorter events, 29.7 us)
Async XLA Ops:
  7.2 61.8 %copy-start = (bf16[256,256]{1,0:T(8,128)(2,1)S(1)}, bf16[256,256]{1,0:T(8,128)(2,1)}, u32[]{:S(2)}) copy-start(bf16[256,256]{1,0:T(8,128)(2,1)} %param.7) | copy-start | bytes 393220
  7.2 34.0 %all-to-all-start.2 = ((bf16[6,128,256]{2,0,1:T(8,128)(2,1)}), bf16[6,128,256]{2,0,1:T(8,128)(2,1)S(1)}, u32[]{:S(2)}, u32[]{:S(2)}) async-start(bf16[6,128,256]{2,0,1:T(8,128)(2,1)} %bitcast.95), calls=%async_computation.2 | async-start | bytes 1048576 | tf_op jit(solution)/shard_map/all_to_all | solution.py:44
  22.9 26.5 %copy-start.2 = (bf16[1,5,256,256]{3,2,1,0:T(8,128)(2,1)S(1)}, bf16[1,5,256,256]{3,2,1,0:T(8,128)(2,1)}, u32[]{:S(2)}) copy-start(bf16[1,5,256,256]{3,2,1,0:T(8,128)(2,1)} %param.6) | copy-start | bytes 1966084
  41.2 17.1 %copy-start.6 = (bf16[256,256]{1,0:T(8,128)(2,1)S(1)}, bf16[256,256]{1,0:T(8,128)(2,1)}, u32[]{:S(2)}) copy-start(bf16[256,256]{1,0:T(8,128)(2,1)} %param.8) | copy-start | bytes 393220
  41.2 27.6 %all-to-all-start = ((bf16[6,128,256]{2,0,1:T(8,128)(2,1)}), bf16[6,128,256]{2,0,1:T(8,128)(2,1)S(1)}, u32[]{:S(2)}, u32[]{:S(2)}) async-start(bf16[6,128,256]{2,0,1:T(8,128)(2,1)} %bitcast), calls=%async_computation | async-start | bytes 1048576 | tf_op jit(solution)/shard_map/all_to_all | solution.py:32
  49.3 727.4 %reduce-scatter.10.cloned.1.call-start = ((), (), s32[]{:S(2)}) async-start(), calls=%async_computation.9 | async-start | bytes 196608
  50.1 745.3 %collective-permute-start.7 = (bf16[256,256]{1,0:T(8,128)(2,1)}, bf16[256,256]{1,0:T(8,128)(2,1)}, u32[]{:S(2)}, u32[]{:S(2)}) collective-permute-start(bf16[256,256]{1,0:T(8,128)(2,1)} %get-tuple-element.8), channel_id=1, source_target_pairs={{0,4},{2,6},{4,0},{6,2},{8,12},{10,14},{12,8},{14,10},{16,20},{18,... | collective-permute-start | bytes 393224 | tf_op jit(solution)/shard_map/ppermute | solution.py:12
  53.1 747.7 %collective-permute-start.9 = (bf16[256,256]{1,0:T(8,128)(2,1)}, bf16[256,256]{1,0:T(8,128)(2,1)}, u32[]{:S(2)}, u32[]{:S(2)}) collective-permute-start(bf16[256,256]{1,0:T(8,128)(2,1)} %get-tuple-element.10), channel_id=1, source_target_pairs={{0,8},{2,10},{4,12},{6,14},{8,0},{10,2},{12,4},{14,6},{16,24},{18,... | collective-permute-start | bytes 393224 | tf_op jit(solution)/shard_map/ppermute | solution.py:12
  54.6 749.7 %collective-permute-start.11 = (bf16[256,256]{1,0:T(8,128)(2,1)}, bf16[256,256]{1,0:T(8,128)(2,1)}, u32[]{:S(2)}, u32[]{:S(2)}) collective-permute-start(bf16[256,256]{1,0:T(8,128)(2,1)} %get-tuple-element.9), channel_id=1, source_target_pairs={{0,16},{2,18},{4,20},{6,22},{8,24},{10,26},{12,28},{14,30},{16,0},... | collective-permute-start | bytes 393224 | tf_op jit(solution)/shard_map/ppermute | solution.py:12
  57.2 739.8 %collective-permute-start.6 = (bf16[768,256]{1,0:T(8,128)(2,1)S(1)}, bf16[768,256]{1,0:T(8,128)(2,1)}, u32[]{:S(2)}, u32[]{:S(2)}) collective-permute-start(bf16[768,256]{1,0:T(8,128)(2,1)S(1)} %all_to_all.63), channel_id=1, source_target_pairs={{0,4},{2,6},{4,0},{6,2},{8,12},{10,14},{12,8},{14,10},{16,20},{18,... | collective-permute-start | bytes 1179656 | tf_op jit(solution)/shard_map/ppermute | solution.py:12
  57.8 743.7 %collective-permute-start.8 = (bf16[768,256]{1,0:T(8,128)(2,1)S(1)}, bf16[768,256]{1,0:T(8,128)(2,1)}, u32[]{:S(2)}, u32[]{:S(2)}) collective-permute-start(bf16[768,256]{1,0:T(8,128)(2,1)S(1)} %all_to_all.63), channel_id=1, source_target_pairs={{0,8},{2,10},{4,12},{6,14},{8,0},{10,2},{12,4},{14,6},{16,24},{18,... | collective-permute-start | bytes 1179656 | tf_op jit(solution)/shard_map/ppermute | solution.py:12
  694.4 99.5 %reduce-scatter.8.cloned.1.call-start = ((), (), s32[]{:S(2)}) async-start(), calls=%async_computation.8 | async-start | bytes 196608 | tf_op jit(solution)/shard_map/reduce_scatter | solution.py:67
  696.9 98.6 %copy-start.11 = (bf16[256,256]{1,0:T(8,128)(2,1)S(1)}, bf16[256,256]{1,0:T(8,128)(2,1)}, u32[]{:S(2)}) copy-start(bf16[256,256]{1,0:T(8,128)(2,1)} %get-tuple-element.7) | copy-start | bytes 393220
  795.5 23.8 %collective-permute-start.5 = (bf16[256,256]{1,0:T(8,128)(2,1)S(1)}, bf16[256,256]{1,0:T(8,128)(2,1)S(1)}, u32[]{:S(2)}, u32[]{:S(2)}) collective-permute-start(bf16[256,256]{1,0:T(8,128)(2,1)S(1)} %copy-done.11), channel_id=1, source_target_pairs={{0,2},{2,0},{4,6},{6,4},{8,10},{10,8},{12,14},{14,12},{16,18},{18,... | collective-permute-start | bytes 393224 | tf_op jit(solution)/shard_map/ppermute | solution.py:12
  797.0 20.4 %collective-permute-start.10 = (bf16[768,256]{1,0:T(8,128)(2,1)S(1)}, bf16[768,256]{1,0:T(8,128)(2,1)S(1)}, u32[]{:S(2)}, u32[]{:S(2)}) collective-permute-start(bf16[768,256]{1,0:T(8,128)(2,1)S(1)} %all_to_all.63), channel_id=1, source_target_pairs={{0,16},{2,18},{4,20},{6,22},{8,24},{10,26},{12,28},{14,30},{16,0},... | collective-permute-start | bytes 1179656 | tf_op jit(solution)/shard_map/ppermute | solution.py:12
  800.8 21.9 %copy-start.1 = (f32[768,256]{1,0:T(8,128)S(1)}, f32[768,256]{1,0:T(8,128)}, u32[]{:S(2)}) copy-start(f32[768,256]{1,0:T(8,128)} %convolution_add_fusion.1) | copy-start | bytes 2359300
  800.8 21.9 %collective-permute-start.4 = (bf16[768,256]{1,0:T(8,128)(2,1)S(1)}, bf16[768,256]{1,0:T(8,128)(2,1)S(1)}, u32[]{:S(2)}, u32[]{:S(2)}) collective-permute-start(bf16[768,256]{1,0:T(8,128)(2,1)S(1)} %all_to_all.63), channel_id=1, source_target_pairs={{0,2},{2,0},{4,6},{6,4},{8,10},{10,8},{12,14},{14,12},{16,18},{18,... | collective-permute-start | bytes 1179656 | tf_op jit(solution)/shard_map/ppermute | solution.py:12
  801.5 33.5 %collective-permute-start = (bf16[768,256]{1,0:T(8,128)(2,1)S(1)}, bf16[768,256]{1,0:T(8,128)(2,1)}, u32[]{:S(2)}, u32[]{:S(2)}) collective-permute-start(bf16[768,256]{1,0:T(8,128)(2,1)S(1)} %all_to_all.55), channel_id=1, source_target_pairs={{0,2},{2,0},{4,6},{6,4},{8,10},{10,8},{12,14},{14,12},{16,18},{18,... | collective-permute-start | bytes 1179656 | tf_op jit(solution)/shard_map/ppermute | solution.py:12
  804.3 32.7 %collective-permute-start.1 = (bf16[768,256]{1,0:T(8,128)(2,1)S(1)}, bf16[768,256]{1,0:T(8,128)(2,1)S(1)}, u32[]{:S(2)}, u32[]{:S(2)}) collective-permute-start(bf16[768,256]{1,0:T(8,128)(2,1)S(1)} %all_to_all.55), channel_id=1, source_target_pairs={{0,4},{2,6},{4,0},{6,2},{8,12},{10,14},{12,8},{14,10},{16,20},{18,... | collective-permute-start | bytes 1179656 | tf_op jit(solution)/shard_map/ppermute | solution.py:12
  817.4 20.7 %collective-permute-start.2 = (bf16[768,256]{1,0:T(8,128)(2,1)S(1)}, bf16[768,256]{1,0:T(8,128)(2,1)S(1)}, u32[]{:S(2)}, u32[]{:S(2)}) collective-permute-start(bf16[768,256]{1,0:T(8,128)(2,1)S(1)} %all_to_all.55), channel_id=1, source_target_pairs={{0,8},{2,10},{4,12},{6,14},{8,0},{10,2},{12,4},{14,6},{16,24},{18,... | collective-permute-start | bytes 1179656 | tf_op jit(solution)/shard_map/ppermute | solution.py:12
  819.2 26.0 %collective-permute-start.3 = (bf16[768,256]{1,0:T(8,128)(2,1)S(1)}, bf16[768,256]{1,0:T(8,128)(2,1)S(1)}, u32[]{:S(2)}, u32[]{:S(2)}) collective-permute-start(bf16[768,256]{1,0:T(8,128)(2,1)S(1)} %all_to_all.55), channel_id=1, source_target_pairs={{0,16},{2,18},{4,20},{6,22},{8,24},{10,26},{12,28},{14,30},{16,0},... | collective-permute-start | bytes 1179656 | tf_op jit(solution)/shard_map/ppermute | solution.py:12
  824.0 33.3 %all-to-all-start.3 = ((bf16[128,6,256]{2,1,0:T(8,128)(2,1)}), bf16[128,6,256]{2,1,0:T(8,128)(2,1)S(1)}, u32[]{:S(2)}, u32[]{:S(2)}) async-start(bf16[128,6,256]{2,1,0:T(8,128)(2,1)} %all_to_all.64), calls=%async_computation.3 | async-start | bytes 1048576 | tf_op jit(solution)/shard_map/all_to_all | solution.py:71
  834.9 47.4 %reduce-scatter.6.cloned.1.call-start = ((), (), s32[]{:S(2)}) async-start(), calls=%async_computation.7 | async-start | bytes 983040 | tf_op jit(solution)/shard_map/reduce_scatter | solution.py:61
  857.2 25.1 %all-to-all-start.1 = ((bf16[128,6,256]{2,1,0:T(8,128)(2,1)}), bf16[128,6,256]{2,1,0:T(8,128)(2,1)S(1)}, u32[]{:S(2)}, u32[]{:S(2)}) async-start(bf16[128,6,256]{2,1,0:T(8,128)(2,1)} %all_to_all.56), calls=%async_computation.1 | async-start | bytes 1048576 | tf_op jit(solution)/shard_map/all_to_all | solution.py:43
  (7 other events, 41.6 us)
Sparse Core Ops, SparseCore 0:
  694.5 82.1 reduce-scatter.9
  779.8 14.1 reduce-scatter.7
  848.7 16.0 reduce-scatter.5
where the time goes:
time: 892 us; the launch traced here: 891 us
  blocking collectives  621 us (70%)
  waiting for transfers between devices  157 us (18%)
  starting transfers between devices  65.8 us (7%)
  matrix products  19 us (2%)
  between operations  14.1 us (2%)
  other arithmetic  9.15 us (1%)
    psum x1, blocking collectives, reduce_latent(): return lax.psum(partial_value, 'hid').astype(jnp.bfloat16)  621 us
    unnamed x4, waiting for transfers between devices  78.5 us
    ppermute x12, starting transfers between devices, swapped(): lax.ppermute(x, axis, [(i, i ^ 1 << stride) for i in range(lax.axis_size(...  21.1 us
  transfers between devices with their start and end apart: 19, of which 8 were waited for; matrix products, arithmetic and copies ran while one was open for 3% of the time, Pallas kernels for 0%

commit v1 on v0

--- a/solution.py
+++ b/solution.py
@@ -16,8 +16,14 @@
     return jax.nn.gelu(value, approximate=True)
 
 
-def reduce_latent(partial_value):
-    return lax.psum(partial_value, "hid").astype(jnp.bfloat16)
+def reduce_latents(first, second):
+    both = jnp.concatenate([first, second], axis=1)
+    rows, wide = both.shape
+    flat = both.reshape(rows * wide // 128, 128)
+    part = lax.psum_scatter(flat, "hid", scatter_dimension=0, tiled=True)
+    full = lax.all_gather(part.astype(jnp.bfloat16), "hid", axis=0, tiled=True)
+    full = full.reshape(rows, wide)
+    return full[:, : wide // 2], full[:, wide // 2 :]
 
 
 def inner_rows(left, right):
@@ -33,7 +39,11 @@
     partners = [act_rows]
     for level in range(LEVELS):
         partners.append(swapped(act_rows, "hid", level))
-    latent = reduce_latent(jnp.dot(act_rows, low_u, preferred_element_type=jnp.float32))
+    grad_rows = lax.all_to_all(grad_out, "hid", split_axis=1, concat_axis=0, tiled=True)
+    latent, dlatent = reduce_latents(
+        jnp.dot(act_rows, low_u, preferred_element_type=jnp.float32),
+        jnp.dot(grad_rows, low_v.T, preferred_element_type=jnp.float32),
+    )
     total = jnp.dot(latent, low_v, preferred_element_type=jnp.float32)
     for level in range(LEVELS + 1):
         total = total + jnp.dot(
@@ -41,8 +51,6 @@
         )
     output_rows = total.astype(jnp.bfloat16)
     output_tok = lax.all_to_all(output_rows, "hid", split_axis=0, concat_axis=1, tiled=True)
-    grad_rows = lax.all_to_all(grad_out, "hid", split_axis=1, concat_axis=0, tiled=True)
-    dlatent = reduce_latent(jnp.dot(grad_rows, low_v.T, preferred_element_type=jnp.float32))
     backward = jnp.dot(dlatent, low_u.T, preferred_element_type=jnp.float32)
     backward = backward + jnp.dot(grad_rows, butterfly[0, 0].T, preferred_element_type=jnp.float32)
     for level in range(1, LEVELS + 1):

time: 892 us -> 1350 us (1.51)
  waiting for transfers between devices: 157 us -> 859 us
  blocking collectives: 621 us -> 341 us
  starting transfers between devices: 65.8 us -> 88.8 us
    unnamed x4 -> x6, waiting for transfers between devices: 78.5 us -> 799 us
    psum x1 -> x0, blocking collectives: 621 us -> none  [reduce_latent(): return lax.psum(partial_value, 'hid').astype(jnp.bfloat16)]
    all_gather x0 -> x1, blocking collectives: none -> 307 us  [reduce_latents(): full = lax.all_gather(part.astype(jnp.bfloat16), 'hid', axis=0, tiled=True)]
    all_to_all x1, starting transfers between devices: 11 us -> 46.1 us  [on_device(): lax.all_to_all(grad_act, 'hid', split_axis=0, concat_axis=1, tiled=True)]
    all_to_all x0 -> x1, blocking collectives: none -> 33.7 us  [on_device(): lax.all_to_all(act_tok, 'hid', split_axis=1, concat_axis=0, tiled=True)]
  transfers between devices with their start and end apart: 19 -> 19, of which waited for: 8 -> 7; matrix products, arithmetic and copies ran while one was open for 3% -> 3% of each run, Pallas kernels for 0% -> 0%
where the time goes in v1:
time: 1350 us
  waiting for transfers between devices  859 us (64%)
  blocking collectives  341 us (25%)
  starting transfers between devices  88.8 us (7%)
  matrix products  20.3 us (2%)
  between operations  14.1 us (1%)
  local copies, waits for them, and re-layouts  14 us (1%)
    unnamed x6, waiting for transfers between devices  799 us
    all_gather x1, blocking collectives, reduce_latents(): full = lax.all_gather(part.astype(jnp.bfloat16), 'hid', axis=0, tiled=True)  307 us
    all_to_all x1, starting transfers between devices, on_device(): lax.all_to_all(grad_act, 'hid', split_axis=0, concat_axis=1, tiled=True)  46.1 us
    all_to_all x1, blocking collectives, on_device(): lax.all_to_all(act_tok, 'hid', split_axis=1, concat_axis=0, tiled=True)  33.7 us
  transfers between devices with their start and end apart: 19, of which 7 were waited for; matrix products, arithmetic and copies ran while one was open for 3% of the time, Pallas kernels for 0%

profile of v1, /device:TPU:2, one launch (start us, length us, event | category | flops | bytes accessed | tf_op | source)
XLA Modules:
  0.0 1346.4 jit_solution(5480149929187112660)
XLA Ops:
  8.6 33.7 %all_to_all.70 = bf16[6,128,256]{2,0,1:T(8,128)(2,1)S(1)} all-to-all(bf16[6,128,256]{2,0,1:T(8,128)(2,1)S(1)} %bitcast.92), channel_id=1, replica_groups=mesh['hid'=128,'seq'=2] {'hid'}, dimensions={1} | all-to-all | bytes 786432 | tf_op jit(solution)/shard_map/all_to_all | solution.py:38
  42.3 7.9 all-to-all-start.1
  50.5 1.6 collective-permute-start
  52.0 2.7 collective-permute-start.1
  56.2 2.4 collective-permute-start.3
  58.6 13.9 %all-to-all-done.1 = bf16[6,128,256]{2,0,1:T(8,128)(2,1)S(1)} async-done(((bf16[6,128,256]{2,0,1:T(8,128)(2,1)}), bf16[6,128,256]{2,0,1:T(8,128)(2,1)S(1)}, u32[]{:S(2)}, u32[]{:S(2)}) %all-to-all-start.1) | async-done | bytes 393248 | tf_op jit(solution)/shard_map/all_to_all | solution.py:42
  76.7 1.5 collective-permute-done.2
  80.7 1.6 copy.19
  82.3 2.5 reshape.108
  86.5 4.3 collective-permute-start.7
  92.7 3.4 collective-permute-start.6
  99.4 5.4 collective-permute-done.6
  109.5 11.6 collective-permute-done.10
  122.2 1.9 convert_element_type.63
  124.1 798.7 %reduce-scatter.15.cloned.1.call-done = f32[24,128]{1,0:T(8,128)} async-done(((f32[3072,128]{1,0:T(8,128)}), f32[24,128]{1,0:T(8,128)}) %reduce-scatter.15.cloned.1.call-update) | async-done | bytes 12304
  923.5 307.2 %all_gather.3 = bf16[3072,128]{1,0:T(8,128)(2,1)S(1)} all-gather(bf16[24,128]{1,0:T(8,128)(2,1)S(1)} %convert_element_type.55), channel_id=1, replica_groups=mesh['hid'=128,'seq'=2] {'hid'}, dimensions={0}, use_global_device_ids=true | all-gather | bytes 792576 | tf_op jit(solution)/shard_map/all_gather | solution.py:24
  1231.5 2.1 convolution_add_fusion.1
  1234.6 1.7 copy.22
  1236.3 2.8 fusion.8
  1239.1 1.9 all_to_all.64
  1241.0 46.1 %all-to-all-start.3 = ((bf16[128,6,256]{2,1,0:T(8,128)(2,1)}), bf16[128,6,256]{2,1,0:T(8,128)(2,1)S(1)}, u32[]{:S(2)}, u32[]{:S(2)}) async-start(bf16[128,6,256]{2,1,0:T(8,128)(2,1)} %all_to_all.64), calls=%async_computation.3 | async-start | bytes 1048576 | tf_op jit(solution)/shard_map/all_to_all | solution.py:79
  1293.7 11.0 reduce-scatter.11.cloned.1.call-done
  1306.2 14.0 %all-to-all-start.2 = ((bf16[128,6,256]{2,1,0:T(8,128)(2,1)}), bf16[128,6,256]{2,1,0:T(8,128)(2,1)S(1)}, u32[]{:S(2)}, u32[]{:S(2)}) async-start(bf16[128,6,256]{2,1,0:T(8,128)(2,1)} %all_to_all.60), calls=%async_computation.2 | async-start | bytes 1048576 | tf_op jit(solution)/shard_map/all_to_all | solution.py:53
  1321.8 17.2 %all-to-all-done.2 = bf16[128,6,256]{2,1,0:T(8,128)(2,1)S(1)} async-done(((bf16[128,6,256]{2,1,0:T(8,128)(2,1)}), bf16[128,6,256]{2,1,0:T(8,128)(2,1)S(1)}, u32[]{:S(2)}, u32[]{:S(2)}) %all-to-all-start.2) | async-done | bytes 393248 | tf_op jit(solution)/shard_map/all_to_all | solution.py:53
  (80 shorter events, 35.3 us)
Async XLA Ops:
  7.2 73.1 %copy-start = (bf16[256,256]{1,0:T(8,128)(2,1)S(1)}, bf16[256,256]{1,0:T(8,128)(2,1)}, u32[]{:S(2)}) copy-start(bf16[256,256]{1,0:T(8,128)(2,1)} %param.7) | copy-start | bytes 393220
  42.3 30.2 %all-to-all-start.1 = ((bf16[6,128,256]{2,0,1:T(8,128)(2,1)}), bf16[6,128,256]{2,0,1:T(8,128)(2,1)S(1)}, u32[]{:S(2)}, u32[]{:S(2)}) async-start(bf16[6,128,256]{2,0,1:T(8,128)(2,1)} %bitcast.3), calls=%async_computation.1 | async-start | bytes 1048576 | tf_op jit(solution)/shard_map/all_to_all | solution.py:42
  50.3 72.0 %reduce-scatter.9.cloned.1.call-start = ((), (), s32[]{:S(2)}) async-start(), calls=%async_computation.8 | async-start | bytes 983040 | tf_op jit(solution)/shard_map/reduce_scatter | solution.py:69
  50.5 24.6 %collective-permute-start = (bf16[768,256]{1,0:T(8,128)(2,1)S(1)}, bf16[768,256]{1,0:T(8,128)(2,1)}, u32[]{:S(2)}, u32[]{:S(2)}) collective-permute-start(bf16[768,256]{1,0:T(8,128)(2,1)S(1)} %all_to_all.55), channel_id=1, source_target_pairs={{0,2},{2,0},{4,6},{6,4},{8,10},{10,8},{12,14},{14,12},{16,18},{18,... | collective-permute-start | bytes 1179656 | tf_op jit(solution)/shard_map/ppermute | solution.py:12
  52.0 24.3 %collective-permute-start.1 = (bf16[768,256]{1,0:T(8,128)(2,1)S(1)}, bf16[768,256]{1,0:T(8,128)(2,1)S(1)}, u32[]{:S(2)}, u32[]{:S(2)}) collective-permute-start(bf16[768,256]{1,0:T(8,128)(2,1)S(1)} %all_to_all.55), channel_id=1, source_target_pairs={{0,4},{2,6},{4,0},{6,2},{8,12},{10,14},{12,8},{14,10},{16,20},{18,... | collective-permute-start | bytes 1179656 | tf_op jit(solution)/shard_map/ppermute | solution.py:12
  54.7 23.5 %collective-permute-start.2 = (bf16[768,256]{1,0:T(8,128)(2,1)S(1)}, bf16[768,256]{1,0:T(8,128)(2,1)S(1)}, u32[]{:S(2)}, u32[]{:S(2)}) collective-permute-start(bf16[768,256]{1,0:T(8,128)(2,1)S(1)} %all_to_all.55), channel_id=1, source_target_pairs={{0,8},{2,10},{4,12},{6,14},{8,0},{10,2},{12,4},{14,6},{16,24},{18,... | collective-permute-start | bytes 1179656 | tf_op jit(solution)/shard_map/ppermute | solution.py:12
  56.2 22.3 %collective-permute-start.3 = (bf16[768,256]{1,0:T(8,128)(2,1)S(1)}, bf16[768,256]{1,0:T(8,128)(2,1)S(1)}, u32[]{:S(2)}, u32[]{:S(2)}) collective-permute-start(bf16[768,256]{1,0:T(8,128)(2,1)S(1)} %all_to_all.55), channel_id=1, source_target_pairs={{0,16},{2,18},{4,20},{6,22},{8,24},{10,26},{12,28},{14,30},{16,0},... | collective-permute-start | bytes 1179656 | tf_op jit(solution)/shard_map/ppermute | solution.py:12
  79.9 842.9 %reduce-scatter.15.cloned.1.call-start = ((), (), s32[]{:S(2)}) async-start(), calls=%async_computation.11 | async-start | bytes 1585152
  84.8 1207.3 %reduce-scatter.13.cloned.1.call-start = ((), (), s32[]{:S(2)}) async-start(), calls=%async_computation.10 | async-start | bytes 196608
  86.5 12.2 collective-permute-start.7
  90.9 16.0 %collective-permute-start.9 = (bf16[256,256]{1,0:T(8,128)(2,1)S(1)}, bf16[256,256]{1,0:T(8,128)(2,1)S(1)}, u32[]{:S(2)}, u32[]{:S(2)}) collective-permute-start(bf16[256,256]{1,0:T(8,128)(2,1)S(1)} %get-tuple-element.8), channel_id=1, source_target_pairs={{0,8},{2,10},{4,12},{6,14},{8,0},{10,2},{12,4},{14,6},{16,24},{18,... | collective-permute-start | bytes 393224 | tf_op jit(solution)/shard_map/ppermute | solution.py:12
  92.2 5.4 copy-start.7
  92.2 17.3 %collective-permute-start.11 = (bf16[256,256]{1,0:T(8,128)(2,1)S(1)}, bf16[256,256]{1,0:T(8,128)(2,1)S(1)}, u32[]{:S(2)}, u32[]{:S(2)}) collective-permute-start(bf16[256,256]{1,0:T(8,128)(2,1)S(1)} %get-tuple-element.7), channel_id=1, source_target_pairs={{0,16},{2,18},{4,20},{6,22},{8,24},{10,26},{12,28},{14,30},{16,0},... | collective-permute-start | bytes 393224 | tf_op jit(solution)/shard_map/ppermute | solution.py:12
  92.7 12.0 collective-permute-start.6
  96.1 12.1 collective-permute-start.8
  98.7 1137.5 %collective-permute-start.5 = (bf16[256,256]{1,0:T(8,128)(2,1)}, bf16[256,256]{1,0:T(8,128)(2,1)S(1)}, u32[]{:S(2)}, u32[]{:S(2)}) collective-permute-start(bf16[256,256]{1,0:T(8,128)(2,1)} %get-tuple-element.5), channel_id=1, source_target_pairs={{0,2},{2,0},{4,6},{6,4},{8,10},{10,8},{12,14},{14,12},{16,18},{18,... | collective-permute-start | bytes 393224 | tf_op jit(solution)/shard_map/ppermute | solution.py:12
  104.7 16.3 %collective-permute-start.10 = (bf16[768,256]{1,0:T(8,128)(2,1)S(1)}, bf16[768,256]{1,0:T(8,128)(2,1)S(1)}, u32[]{:S(2)}, u32[]{:S(2)}) collective-permute-start(bf16[768,256]{1,0:T(8,128)(2,1)S(1)} %all_to_all.59), channel_id=1, source_target_pairs={{0,16},{2,18},{4,20},{6,22},{8,24},{10,26},{12,28},{14,30},{16,0},... | collective-permute-start | bytes 1179656 | tf_op jit(solution)/shard_map/ppermute | solution.py:12
  106.8 1129.4 %collective-permute-start.4 = (bf16[768,256]{1,0:T(8,128)(2,1)S(1)}, bf16[768,256]{1,0:T(8,128)(2,1)}, u32[]{:S(2)}, u32[]{:S(2)}) collective-permute-start(bf16[768,256]{1,0:T(8,128)(2,1)S(1)} %all_to_all.59), channel_id=1, source_target_pairs={{0,2},{2,0},{4,6},{6,4},{8,10},{10,8},{12,14},{14,12},{16,18},{18,... | collective-permute-start | bytes 1179656 | tf_op jit(solution)/shard_map/ppermute | solution.py:12
  1233.6 2.7 copy-start.3
  1241.0 65.2 %all-to-all-start.3 = ((bf16[128,6,256]{2,1,0:T(8,128)(2,1)}), bf16[128,6,256]{2,1,0:T(8,128)(2,1)S(1)}, u32[]{:S(2)}, u32[]{:S(2)}) async-start(bf16[128,6,256]{2,1,0:T(8,128)(2,1)} %all_to_all.64), calls=%async_computation.3 | async-start | bytes 1048576 | tf_op jit(solution)/shard_map/all_to_all | solution.py:79
  1287.1 17.7 %reduce-scatter.11.cloned.1.call-start = ((), (), s32[]{:S(2)}) async-start(), calls=%async_computation.9 | async-start | bytes 196608 | tf_op jit(solution)/shard_map/reduce_scatter | solution.py:75
  1288.4 1.4 copy-start.2
  1306.2 14.1 %copy-start.5 = (bf16[6,32768]{1,0:T(8,128)(2,1)S(1)}, bf16[6,32768]{1,0:T(8,128)(2,1)}, u32[]{:S(2)}) copy-start(bf16[6,32768]{1,0:T(8,128)(2,1)} %param.5) | copy-start | bytes 1179652
  1306.2 32.9 %all-to-all-start.2 = ((bf16[128,6,256]{2,1,0:T(8,128)(2,1)}), bf16[128,6,256]{2,1,0:T(8,128)(2,1)S(1)}, u32[]{:S(2)}, u32[]{:S(2)}) async-start(bf16[128,6,256]{2,1,0:T(8,128)(2,1)} %all_to_all.60), calls=%async_computation.2 | async-start | bytes 1048576 | tf_op jit(solution)/shard_map/all_to_all | solution.py:53
  (4 other events, 4.8 us)
Sparse Core Ops, SparseCore 0:
  80.0 13.5 reduce-scatter.8
  99.0 823.7 reduce-scatter.14
  1236.4 43.7 reduce-scatter.12
  1290.6 14.0 reduce-scatter.10

commit v2 on v0

v2 whole, which is shorter than its diff:
```python
import functools
import math

import jax
import jax.numpy as jnp
from jax import lax
from jax.experimental import pallas as pl
from jax.experimental.pallas import tpu as pltpu
from jax.sharding import Mesh
from jax.sharding import PartitionSpec as P

MESH = pl.DeviceIdType.MESH
BF, F32 = jnp.bfloat16, jnp.float32
GROUPS = 32
FACTOR = 1.0 / math.sqrt(1536)


def flip(value, bit):
    step = 1 << bit
    return value + step - 2 * step * lax.rem(lax.div(value, step), 2)


def dot(a, b):
    return jnp.dot(a, b, preferred_element_type=F32)


def dot_t(a, b):
    return lax.dot_general(a, b, (((1,), (1,)), ((), ())), preferred_element_type=F32)


def t_dot(a, b):
    return lax.dot_general(a, b, (((0,), (0,)), ((), ())), preferred_element_type=F32)


def cols(start, size, unit):
    return pl.ds(pl.multiple_of(start, unit), size)


def kernel(
    act, grad, bfly, low_u, low_v,
    out_tok, gact_tok, wg_out,
    A, G, G1, G2, W, acc_o, acc_g, stage, lat_send, lat_recv, lat_own, lat_all,
    wg_send, wg_recv, send_sem, recv_sem,
):
    x, z, y, c = (lax.axis_index(n) for n in ("x", "z", "y", "seq"))
    me = x * 8 + z
    sib = 1 - c
    mine, other = cols(c * 128, 128, 128), cols(sib * 128, 128, 128)
    z1, z2 = flip(z, 0), flip(z, 1)

    def remote(src, dst, ch, **dev):
        pltpu.make_async_remote_copy(
            src_ref=src, dst_ref=dst, send_sem=send_sem.at[ch], recv_sem=recv_sem.at[ch],
            device_id=dev, device_id_type=MESH,
        ).start()

    def local(src, dst, ch):
        pltpu.make_async_copy(src, dst, recv_sem.at[ch]).start()

    def arrived(ref, ch):
        pltpu.make_async_copy(ref, ref, recv_sem.at[ch]).wait()

    def sent(ref, ch):
        pltpu.make_async_copy(ref, ref, send_sem.at[ch]).wait()

    def peer(d):
        q = lax.rem(me + d, GROUPS)
        return q, lax.div(q, 8), lax.rem(q, 8)

    def ypeer(d):
        return lax.rem(y + d, 4)

    barrier = pltpu.get_barrier_semaphore()

    @pl.loop(1, GROUPS)
    def _(d):
        q, qx, qz = peer(d)
        pl.semaphore_signal(barrier, 1, device_id={"x": qx, "z": qz}, device_id_type=MESH)

    for d in range(1, 4):
        pl.semaphore_signal(barrier, 1, device_id={"y": ypeer(d)}, device_id_type=MESH)
    pl.semaphore_signal(barrier, 1, device_id={"seq": sib}, device_id_type=MESH)
    pl.semaphore_wait(barrier, GROUPS + 3)

    def scatter(src, dst, ch):
        @pl.loop(1, GROUPS)
        def _(d):
            q, qx, qz = peer(d)
            remote(src.at[q], dst.at[me], ch, x=qx, z=qz)

        local(src.at[me], dst.at[me], ch)

    scatter(grad, G.at[c], 0)
    local(bfly, W.at[y, pl.ds(0, 5)], 1)
    local(low_u, W.at[y, 5], 1)
    local(low_v, W.at[y, 6], 1)
    remote(bfly.at[3, mine], W.at[y, 7, mine], 2, z=z1)
    remote(bfly.at[4, mine], W.at[y, 8, mine], 3, z=z2)
    for d in range(1, 4):
        remote(low_u.at[mine], W.at[y, 5, mine], 3 + d, y=ypeer(d))
        remote(low_v.at[mine], W.at[y, 6, mine], 3 + d, y=ypeer(d))
        remote(bfly.at[:, mine], W.at[y, pl.ds(0, 5), mine], 3 + d, y=ypeer(d))
    scatter(act, A.at[0, c], 7)

    arrived(W.at[y, 7, mine], 2)
    arrived(W.at[y, 8, mine], 3)
    far = pl.ds(7, 2)
    for d in range(1, 4):
        remote(W.at[y, far, mine], W.at[y, far, mine], 7 + d, y=ypeer(d))
    remote(W.at[y, far, mine], W.at[y, far, mine], 11, seq=sib)

    arrived(G.at[c], 0)
    remote(G.at[c], G1, 12, z=z1)
    remote(G.at[c], G2, 13, z=z2)
    remote(G.at[c], G.at[c], 14, seq=sib)
    arrived(A.at[0, c], 7)
    remote(A.at[0, c], A.at[1, c], 15, z=z1)
    remote(A.at[0, c], A.at[2, c], 16, z=z2)
    remote(A.at[0, c], A.at[0, c], 17, seq=sib)

    near = pl.ds(0, 7)
    for d in range(1, 4):
        ys = ypeer(4 - d)
        arrived(W.at[ys, near, mine], 3 + d)
        remote(W.at[ys, near, mine], W.at[ys, near, mine], 17 + d, seq=sib)
    arrived(W.at[y, near], 1)
    for d in range(1, 4):
        arrived(W.at[ypeer(4 - d), near, other], 17 + d)

    def block(ref, b):
        return ref[:, :, :, cols(b * 256, 256, 256)].reshape(192, 256)

    A0, G0 = A.at[0, c], G.at[c]

    lat = dlat = None
    for b in range(4):
        u = dot(block(A0, b), W[b, 5])
        v = dot_t(block(G0, b), W[b, 6])
        lat, dlat = (u, v) if b == 0 else (lat + u, dlat + v)
    lat_send[:, :, :, 0:256] = lat.astype(BF).reshape(GROUPS, 3, 2, 256)
    lat_send[:, :, :, 256:512] = dlat.astype(BF).reshape(GROUPS, 3, 2, 256)
    scatter(lat_send, lat_recv, 21)

    for d in range(1, 4):
        ys = ypeer(4 - d)
        arrived(W.at[ys, far, mine], 7 + d)
        remote(W.at[ys, far, mine], W.at[ys, far, mine], 21 + d, seq=sib)

    @pl.loop(0, 4)
    def _(b):
        b1, b2 = flip(b, 0), flip(b, 1)
        here = cols(b * 256, 256, 256)
        acc_o[:, here] = (
            dot(block(A0, b), W[b, 0]) + dot(block(A0, b1), W[b, 1]) + dot(block(A0, b2), W[b, 2])
        )
        acc_g[:, here] = (
            dot_t(block(G0, b), W[b, 0])
            + dot_t(block(G0, b1), W[b1, 1])
            + dot_t(block(G0, b2), W[b2, 2])
        )

    arrived(lat_recv, 21)
    total = lat_recv[0].astype(F32)
    for q in range(1, GROUPS):
        total = total + lat_recv[q].astype(F32)
    lat_own[...] = total.astype(BF)

    @pl.loop(1, GROUPS)
    def _(d):
        q, qx, qz = peer(d)
        remote(lat_own, lat_all.at[c, me], 25, x=qx, z=qz)

    local(lat_own, lat_all.at[c, me], 25)

    arrived(G1, 12)
    arrived(G2, 13)
    arrived(A.at[1, c], 15)
    remote(A.at[1, c], A.at[1, c], 26, seq=sib)
    arrived(A.at[2, c], 16)
    remote(A.at[2, c], A.at[2, c], 27, seq=sib)
    arrived(W.at[y, far, other], 11)
    for d in range(1, 4):
        arrived(W.at[ypeer(4 - d), far, other], 21 + d)
    A1, A2 = A.at[1, c], A.at[2, c]

    arrived(lat_all.at[c], 25)
    remote(lat_all.at[c], lat_all.at[c], 28, seq=sib)
    pair = lat_all[c].reshape(192, 512)

    @pl.loop(0, 4)
    def _(b):
        here = cols(b * 256, 256, 256)
        o = (
            acc_o[:, here] + dot(block(A1, b), W[b, 3]) + dot(block(A2, b), W[b, 4])
            + dot(pair[:, 0:256], W[b, 6])
        )
        stage[0, :, :, :, here] = o.astype(BF).reshape(GROUPS, 3, 2, 256)
        g = (
            acc_g[:, here] + dot_t(block(G1, b), W[b, 7]) + dot_t(block(G2, b), W[b, 8])
            + dot_t(pair[:, 256:512], W[b, 5])
        )
        stage[1, :, :, :, here] = g.astype(BF).reshape(GROUPS, 3, 2, 256)

    for which, ref in ((0, out_tok), (1, gact_tok)):
        @pl.loop(1, GROUPS)
        def _(d):
            q, qx, qz = peer(d)
            remote(stage.at[which, q], ref.at[me], 29 + which, x=qx, z=qz)

        local(stage.at[which, me], ref.at[me], 29 + which)

    arrived(G.at[sib], 14)
    arrived(A.at[0, sib], 17)
    arrived(A.at[1, sib], 26)
    arrived(A.at[2, sib], 27)
    arrived(lat_all.at[sib], 28)
    lat_half = lat_all[:, :, :, :, cols(c * 128, 128, 128)].reshape(384, 128)
    dlat_half = lat_all[:, :, :, :, cols(256 + c * 128, 128, 128)].reshape(384, 128)

    def half(level, b):
        return A[level, :, :, :, :, cols(b * 256 + c * 128, 128, 128)].reshape(384, 128)

    for d in range(4):
        b = ypeer(d)
        whole = cols(b * 256, 256, 256)
        g = G[:, :, :, :, whole].reshape(384, 256)
        a = A[0, :, :, :, :, whole].reshape(384, 256)
        sums = [
            t_dot(half(0, b), g),
            t_dot(half(0, flip(b, 0)), g),
            t_dot(half(0, flip(b, 1)), g),
            t_dot(half(1, b), g),
            t_dot(half(2, b), g),
            t_dot(dlat_half, a),
            t_dot(lat_half, g),
        ]
        for k, value in enumerate(sums):
            if d == 0:
                wg_out[k] = value * FACTOR
            else:
                wg_send[d - 1, k] = (value * FACTOR).astype(BF)
        if d:
            remote(wg_send.at[d - 1], wg_recv.at[d - 1], 30 + d, y=b)
    for d in range(1, 4):
        arrived(wg_recv.at[d - 1], 30 + d)
        for k in range(7):
            wg_out[k] = wg_out[k] + wg_recv[d - 1, k].astype(F32)
    arrived(stage.at[0], 29)
    arrived(stage.at[1], 30)

    most = pl.ds(0, GROUPS - 1)
    sent(G.at[0, most], 0)
    sent(W.at[0, 7, pl.ds(0, 128)], 2)
    sent(W.at[0, 8, pl.ds(0, 128)], 3)
    for d in range(1, 4):
        sent(W.at[0, near, pl.ds(0, 128)], 3 + d)
        sent(W.at[0, far, pl.ds(0, 128)], 7 + d)
        sent(W.at[0, near, pl.ds(0, 128)], 17 + d)
        sent(W.at[0, far, pl.ds(0, 128)], 21 + d)
        sent(wg_send.at[d - 1], 30 + d)
    sent(W.at[0, far, pl.ds(0, 128)], 11)
    sent(A.at[0, 0, most], 7)
    for ch in (12, 13, 14, 15, 16, 17, 26, 27):
        sent(G.at[0], ch)
    sent(lat_send.at[most], 21)
    sent(lat_all.at[0, most], 25)
    sent(lat_all.at[0], 28)
    sent(stage.at[0, most], 29)
    sent(stage.at[1, most], 30)


def exchange(act, grad, bfly, low_u, low_v):
    tok = (GROUPS, 3, 2, 1024)
    any_space = pl.BlockSpec(memory_space=pl.ANY)
    vmem = pl.BlockSpec(memory_space=pltpu.VMEM)
    return pl.pallas_call(
        kernel,
        out_shape=(
            jax.ShapeDtypeStruct(tok, BF),
            jax.ShapeDtypeStruct(tok, BF),
            jax.ShapeDtypeStruct((7, 128, 256), F32),
        ),
        in_specs=[any_space] * 5,
        out_specs=(any_space, any_space, vmem),
        scratch_shapes=[
            pltpu.VMEM((3, 2) + tok, BF),
            pltpu.VMEM((2,) + tok, BF),
            pltpu.VMEM(tok, BF),
            pltpu.VMEM(tok, BF),
            pltpu.VMEM((4, 9, 256, 256), BF),
            pltpu.VMEM((192, 1024), F32),
            pltpu.VMEM((192, 1024), F32),
            pltpu.VMEM((2,) + tok, BF),
            pltpu.VMEM((GROUPS, 3, 2, 512), BF),
            pltpu.VMEM((GROUPS, 3, 2, 512), BF),
            pltpu.VMEM((3, 2, 512), BF),
            pltpu.VMEM((2, GROUPS, 3, 2, 512), BF),
            pltpu.VMEM((3, 7, 128, 256), BF),
            pltpu.VMEM((3, 7, 128, 256), BF),
            pltpu.SemaphoreType.DMA((34,)),
            pltpu.SemaphoreType.DMA((34,)),
        ],
        compiler_params=pltpu.CompilerParams(
            collective_id=0, has_side_effects=True, vmem_limit_bytes=48 * 2**20
        ),
    )(act, grad, bfly, low_u, low_v)


def gelu_tanh(value):
    return jax.nn.gelu(value, approximate=True)


def by_group(rows):
    return rows.reshape(3, 2, GROUPS, 1024).transpose(2, 0, 1, 3)


def by_token(groups):
    return groups.transpose(1, 2, 0, 3).reshape(6, 32768)


def on_device(pre_act, butterfly, low_u, low_v, grad_out):
    pre_f = pre_act.astype(F32)
    act_tok = gelu_tanh(pre_f).astype(BF)
    out_g, gact_g, wg = exchange(
        by_group(act_tok), by_group(grad_out), butterfly[0], low_u, low_v
    )
    unused, pullback = jax.vjp(gelu_tanh, pre_f)
    grad_pre = pullback(by_token(gact_g).astype(F32))[0].astype(BF)
    return by_token(out_g), grad_pre, wg[None, 0:5], wg[5].T, wg[6]


def solution(mesh):
    whole = Mesh(mesh.devices.reshape(4, 8, 4, 2), ("x", "z", "y", "seq"))
    hid = ("x", "z", "y")
    tokens = P(hid + ("seq",), None)
    return jax.shard_map(
        on_device,
        mesh=whole,
        in_specs=(tokens, P(hid, None, None, None), P(hid, None), P(None, hid), tokens),
        out_specs=(tokens, tokens, P(hid, None, "seq", None), P(hid, "seq"), P("seq", hid)),
        check_vma=False,
    )
```

time: 892 us -> 117 us (0.13)
  blocking collectives: 621 us -> 0 us
  waiting for transfers between devices: 157 us -> 0 us
  Pallas kernels: 0 us -> 105 us
  starting transfers between devices: 65.8 us -> 0 us
  matrix products: 19 us -> 0 us
  between operations: 14.1 us -> 0.72 us
    psum x1 -> x0, blocking collectives: 621 us -> none  [reduce_latent(): return lax.psum(partial_value, 'hid').astype(jnp.bfloat16)]
    pallas_call x0 -> x1, Pallas kernels: none -> 105 us  [exchange(): pl.pallas_call(kernel, out_shape=(jax.ShapeDtypeStruct(tok, BF), jax.Shap...]
    unnamed x4 -> x0, waiting for transfers between devices: 78.5 us -> none
    all_to_all x4 -> x0, waiting for transfers between devices: 46.6 us -> none  [the longest x1 17.2 us: on_device(): lax.all_to_all(grad_out, 'hid', split_axis=1, concat_axis=0, tiled=True)]
    all_to_all x4 -> x0, starting transfers between devices: 44.5 us -> none  [the longest x1 15.7 us: on_device(): lax.all_to_all(grad_out, 'hid', split_axis=1, concat_axis=0, tiled=True)]
    ppermute x12 -> x0, starting transfers between devices: 21.1 us -> none  [swapped(): lax.ppermute(x, axis, [(i, i ^ 1 << stride) for i in range(lax.axis_size(...]
    dot_general x21 -> x0, matrix products: 19 us -> none  [the longest x7 7.35 us: inner_rows(): lax.dot_general(left, right, (((0,), (0,)), ((), ())), preferred_element_...]
    ppermute x12 -> x0, waiting for transfers between devices: 16.4 us -> none  [swapped(): lax.ppermute(x, axis, [(i, i ^ 1 << stride) for i in range(lax.axis_size(...]
  transfers between devices with their start and end apart: 19 -> 0, of which waited for: 8 -> 0; matrix products, arithmetic and copies ran while one was open for 3% -> 0% of each run, Pallas kernels for 0% -> 0%
where the time goes in v2:
time: 117 us; the launch traced here: 116 us
  Pallas kernels  105 us (90%)
  local copies, waits for them, and re-layouts  7.05 us (6%)
  other arithmetic  3.21 us (3%)
    pallas_call x1, Pallas kernels, exchange(): pl.pallas_call(kernel, out_shape=(jax.ShapeDtypeStruct(tok, BF), jax.Shap...  105 us
    unnamed x15, local copies, waits for them, and re-layouts  4.35 us

profile of v2, /device:TPU:2, one launch (start us, length us, event | category | flops | bytes accessed | tf_op | source)
XLA Modules:
  0.0 116.4 jit_solution(13495611746243150737)
XLA Ops:
  0.6 1.4 %fusion.7 = bf16[6,32768]{1,0:T(8,128)(2,1)S(1)} fusion(bf16[6,32768]{1,0:T(8,128)(2,1)} %param.5), kind=kLoop, calls=%fused_computation.12 | loop fusion | flops 1966080 | bytes 786432 | tf_op jit(solution)/shard_map/convert_element_type | solution.py:323
  2.0 0.0 copy-start.4
  2.1 0.2 copy.16
  2.3 0.8 copy-done.4
  3.1 0.2 copy.17
  3.3 0.0 copy-start
  3.3 0.0 copy-start.1
  3.3 0.0 copy-start.2
  3.3 0.8 copy_bitcast_fusion
  4.2 0.2 copy-done
  4.4 0.0 copy-done.1
  4.4 0.0 copy-done.2
  4.5 105.4 %shard_map.92 = (bf16[32,3,2,1024]{3,2,1,0:T(2,128)(2,1)S(1)}, bf16[32,3,2,1024]{3,2,1,0:T(2,128)(2,1)S(1)}, f32[7,128,256]{2,1,0:T(8,128)S(1)}) custom-call(bf16[32,3,2,1024]{3,2,1,0:T(2,128)(2,1)S(1)} %get-tuple-element.24.act, bf16[32,3,2,1024]{3,2,1,0:T(2,128)(2,1)S(1)} %get-tuple-element.23.grad, bf16[5,256,256]{2,1,0:T(8,128)(2,1)S(1)} %bitcast.28, ...), custom_call_target="tpu_custom_call" | custom-call | tf_op jit(solution)/shard_map/pallas_call | solution.py:276
  109.8 0.7 slice_bitcast_fusion.1
  110.5 0.8 copy.15
  111.3 0.9 slice_bitcast_fusion
  112.1 0.3 convert_bitcast_fusion
  112.4 0.3 copy.14
  112.7 0.0 copy-start.3
  112.7 0.5 copy.19
  113.2 0.5 copy-done.3
  113.7 1.5 %fusion.3 = bf16[6,32768]{1,0:T(8,128)(2,1)} fusion(bf16[6,32768]{1,0:T(8,128)(2,1)S(1)} %copy-done.3, f32[6,32768]{1,0:T(8,128)S(1)} %bitcast.30), kind=kLoop, calls=%fused_computation.8 | loop fusion | flops 4128768 | bytes 1572864 | tf_op jit(solution)/shard_map/convert_element_type | solution.py:328
  115.3 0.1 copy.13
  115.3 1.0 copy.18
Async XLA Ops:
  2.0 1.0 copy-start.4
  3.3 1.1 copy-start
  3.3 1.1 copy-start.1
  3.3 1.1 copy-start.2
  112.7 1.0 copy-start.3

commit v3 on v2

v3 whole, which is shorter than its diff:
```python
import functools
import math

import jax
import jax.numpy as jnp
from jax import lax
from jax.experimental import pallas as pl
from jax.experimental.pallas import tpu as pltpu
from jax.sharding import Mesh
from jax.sharding import PartitionSpec as P

MESH = pl.DeviceIdType.MESH
BF, F32 = jnp.bfloat16, jnp.float32
GROUPS = 32
FACTOR = 1.0 / math.sqrt(1536)


def flip(value, bit):
    step = 1 << bit
    return value + step - 2 * step * lax.rem(lax.div(value, step), 2)


def dot(a, b):
    return jnp.dot(a, b, preferred_element_type=F32)


def dot_t(a, b):
    return lax.dot_general(a, b, (((1,), (1,)), ((), ())), preferred_element_type=F32)


def t_dot(a, b):
    return lax.dot_general(a, b, (((0,), (0,)), ((), ())), preferred_element_type=F32)


def cols(start, size, unit):
    return pl.ds(pl.multiple_of(start, unit), size)


CHANNELS = (
    "g", "a", "own", "zfar3", "zfar4", "g1", "g2", "gsib", "asib0", "asib1", "asib2", "farsib",
    "latz", "bcz", "latsib", "out", "gact", "a1h0", "a1h1", "a2h0", "a2h1",
) + tuple(
    name + str(d)
    for name in ("low", "lows", "fly", "flys", "far", "fars", "latx", "bcx", "wa", "wb", "wc")
    for d in (1, 2, 3)
)
CH = {name: i for i, name in enumerate(CHANNELS)}


def kernel(
    act, grad, bfly, low_u, low_v,
    out_tok, gact_tok, wg_out,
    A, G, DA, DG, DG1, DG2, W, acc_o, acc_g, stage, lat_send, latx_recv, latx, latz_recv,
    lat_own, lat_all, wg_send, wg_recv, send_sem, recv_sem,
):
    x, z, y, c = (lax.axis_index(n) for n in ("x", "z", "y", "seq"))
    me = x * 8 + z
    sib = 1 - c
    mine, other = cols(c * 128, 128, 128), cols(sib * 128, 128, 128)
    z1, z2 = flip(z, 0), flip(z, 1)

    def remote(src, dst, ch, **dev):
        pltpu.make_async_remote_copy(
            src_ref=src, dst_ref=dst, send_sem=send_sem.at[CH[ch]], recv_sem=recv_sem.at[CH[ch]],
            device_id=dev, device_id_type=MESH,
        ).start()

    def local(src, dst, ch):
        pltpu.make_async_copy(src, dst, recv_sem.at[CH[ch]]).start()

    def arrived(ref, ch):
        pltpu.make_async_copy(ref, ref, recv_sem.at[CH[ch]]).wait()

    def sent(ref, ch):
        pltpu.make_async_copy(ref, ref, send_sem.at[CH[ch]]).wait()

    def peer(d):
        q = lax.rem(me + d, GROUPS)
        return q, lax.div(q, 8), lax.rem(q, 8)

    def ypeer(d):
        return lax.rem(y + d, 4)

    def xpeer(d):
        return lax.rem(x + d, 4)

    def xrows(xv):
        return pl.ds(xv * 8, 8)

    barrier = pltpu.get_barrier_semaphore()

    @pl.loop(1, GROUPS)
    def _(d):
        q, qx, qz = peer(d)
        pl.semaphore_signal(barrier, 1, device_id={"x": qx, "z": qz}, device_id_type=MESH)

    for d in range(1, 4):
        pl.semaphore_signal(barrier, 1, device_id={"y": ypeer(d)}, device_id_type=MESH)
    pl.semaphore_signal(barrier, 1, device_id={"seq": sib}, device_id_type=MESH)
    pl.semaphore_wait(barrier, GROUPS + 3)

    def scatter(src, dst, ch):
        @pl.loop(1, GROUPS)
        def _(d):
            q, qx, qz = peer(d)
            remote(src.at[q], dst.at[me], ch, x=qx, z=qz)

        local(src.at[me], dst.at[me], ch)

    fly, low, far = pl.ds(0, 5), pl.ds(5, 2), pl.ds(7, 2)
    scatter(grad, G.at[0], "g")
    local(bfly, W.at[y, fly], "own")
    local(low_u, W.at[y, 5], "own")
    local(low_v, W.at[y, 6], "own")
    for d in range(1, 4):
        remote(low_u.at[mine], W.at[y, 5, mine], f"low{d}", y=ypeer(d))
        remote(low_v.at[mine], W.at[y, 6, mine], f"low{d}", y=ypeer(d))
    remote(bfly.at[3, mine], W.at[y, 7, mine], "zfar3", z=z1)
    remote(bfly.at[4, mine], W.at[y, 8, mine], "zfar4", z=z2)
    scatter(act, A.at[0], "a")
    for d in range(1, 4):
        remote(bfly.at[:, mine], W.at[y, fly, mine], f"fly{d}", y=ypeer(d))

    for d in range(1, 4):
        ys = ypeer(4 - d)
        arrived(W.at[ys, low, mine], f"low{d}")
        remote(W.at[ys, low, mine], W.at[ys, low, mine], f"lows{d}", seq=sib)

    def dense(raw, out):
        @pl.loop(0, 4)
        def _(b):
            here = cols(b * 256, 256, 256)
            out[:, here] = raw[:, :, :, here].reshape(192, 256)

    arrived(G.at[0], "g")
    remote(G.at[0], G.at[2], "g2", z=z2)
    remote(G.at[0], G.at[1], "g1", z=z1)
    dense(G.at[0], DG.at[c])
    remote(DG.at[c], DG.at[c], "gsib", seq=sib)

    arrived(W.at[y, 7, mine], "zfar3")
    arrived(W.at[y, 8, mine], "zfar4")
    for d in range(1, 4):
        remote(W.at[y, far, mine], W.at[y, far, mine], f"far{d}", y=ypeer(d))
    remote(W.at[y, far, mine], W.at[y, far, mine], "farsib", seq=sib)

    arrived(A.at[0], "a")
    dense(A.at[0], DA.at[0, c])
    remote(DA.at[0, c], DA.at[0, c], "asib0", seq=sib)
    A0, G0 = DA.at[0, c], DG.at[c]

    arrived(W.at[y, pl.ds(0, 7)], "own")
    for d in range(1, 4):
        arrived(W.at[ypeer(4 - d), low, other], f"lows{d}")
    lat = dlat = None
    for b in range(4):
        u = dot(A0[:, b * 256 : b * 256 + 256], W[b, 5])
        v = dot_t(G0[:, b * 256 : b * 256 + 256], W[b, 6])
        lat, dlat = (u, v) if b == 0 else (lat + u, dlat + v)
    lat_send[:, :, :, 0:256] = lat.astype(BF).reshape(GROUPS, 3, 2, 256)
    lat_send[:, :, :, 256:512] = dlat.astype(BF).reshape(GROUPS, 3, 2, 256)
    for d in range(1, 4):
        remote(lat_send.at[xrows(xpeer(d))], latx_recv.at[d - 1], f"latx{d}", x=xpeer(d))

    for d in range(1, 4):
        ys = ypeer(4 - d)
        arrived(W.at[ys, fly, mine], f"fly{d}")
        remote(W.at[ys, fly, mine], W.at[ys, fly, mine], f"flys{d}", seq=sib)

    total = lat_send[xrows(x)].astype(F32)
    for d in range(1, 4):
        arrived(latx_recv.at[d - 1], f"latx{d}")
        total = total + latx_recv[d - 1].astype(F32)
    latx[...] = total.astype(BF)
    for d in range(1, 8):
        zp = lax.rem(z + d, 8)
        remote(latx.at[zp], latz_recv.at[z], "latz", z=zp)
    local(latx.at[z], latz_recv.at[z], "latz")

    first, second = pl.ds(0, 16), pl.ds(16, 16)
    remote(A.at[0, first], A.at[2, first], "a2h0", z=z2)
    remote(A.at[0, first], A.at[1, first], "a1h0", z=z1)

    for d in range(1, 4):
        arrived(W.at[ypeer(4 - d), fly, other], f"flys{d}")

    @pl.loop(0, 4)
    def _(b):
        b1, b2 = flip(b, 0), flip(b, 1)
        h0, h1, h2 = (cols(v * 256, 256, 256) for v in (b, b1, b2))
        acc_o[:, h0] = dot(A0[:, h0], W[b, 0]) + dot(A0[:, h1], W[b, 1]) + dot(A0[:, h2], W[b, 2])
        acc_g[:, h0] = (
            dot_t(G0[:, h0], W[b, 0]) + dot_t(G0[:, h1], W[b1, 1]) + dot_t(G0[:, h2], W[b2, 2])
        )

    arrived(latz_recv, "latz")
    total = latz_recv[0].astype(F32)
    for q in range(1, 8):
        total = total + latz_recv[q].astype(F32)
    lat_own[...] = total.astype(BF)
    for d in range(1, 8):
        remote(lat_own, lat_all.at[c, me], "bcz", z=lax.rem(z + d, 8))
    local(lat_own, lat_all.at[c, me], "bcz")
    remote(A.at[0, second], A.at[2, second], "a2h1", z=z2)
    remote(A.at[0, second], A.at[1, second], "a1h1", z=z1)

    def half(level, b):
        return DA[level, :, :, cols(b * 256 + c * 128, 128, 128)].reshape(384, 128)

    def gblock(b):
        return DG[:, :, cols(b * 256, 256, 256)].reshape(384, 256)

    def keep(d, k, value):
        if d == 0:
            wg_out[k] = value * FACTOR
        else:
            wg_send[d - 1, k] = (value * FACTOR).astype(BF)

    def ship(d, name, rows):
        if d:
            remote(wg_send.at[d - 1, rows], wg_recv.at[d - 1, rows], f"{name}{d}", y=ypeer(d))

    part_a, part_b, part_c = pl.ds(0, 3), pl.ds(5, 2), pl.ds(3, 2)
    arrived(DG.at[sib], "gsib")
    arrived(DA.at[0, sib], "asib0")
    for d in (2, 1, 3, 0):
        b = ypeer(d)
        g = gblock(b)
        keep(d, 0, t_dot(half(0, b), g))
        keep(d, 1, t_dot(half(0, flip(b, 0)), g))
        keep(d, 2, t_dot(half(0, flip(b, 1)), g))
        ship(d, "wa", part_a)

    for d in range(1, 4):
        ys = ypeer(4 - d)
        arrived(W.at[ys, far, mine], f"far{d}")
        remote(W.at[ys, far, mine], W.at[ys, far, mine], f"fars{d}", seq=sib)

    arrived(lat_all.at[c, xrows(x)], "bcz")
    for d in range(1, 4):
        rows = xrows(x)
        remote(lat_all.at[c, rows], lat_all.at[c, rows], f"bcx{d}", x=xpeer(d))

    arrived(G.at[1], "g1")
    dense(G.at[1], DG1)
    arrived(G.at[2], "g2")
    dense(G.at[2], DG2)
    arrived(W.at[y, far, other], "farsib")
    for d in range(1, 4):
        arrived(W.at[ypeer(4 - d), far, other], f"fars{d}")
    for d in range(1, 4):
        arrived(lat_all.at[c, xrows(xpeer(4 - d))], f"bcx{d}")
    remote(lat_all.at[c], lat_all.at[c], "latsib", seq=sib)
    pair = lat_all[c].reshape(192, 512)

    @pl.loop(0, 4)
    def _(b):
        here = cols(b * 256, 256, 256)
        g = (
            acc_g[:, here] + dot_t(DG1[:, here], W[b, 7]) + dot_t(DG2[:, here], W[b, 8])
            + dot_t(pair[:, 256:512], W[b, 5])
        )
        stage[1, :, :, :, here] = g.astype(BF).reshape(GROUPS, 3, 2, 256)

    def gather(which, ref, ch):
        @pl.loop(1, GROUPS)
        def _(d):
            q, qx, qz = peer(d)
            remote(stage.at[which, q], ref.at[me], ch, x=qx, z=qz)

        local(stage.at[which, me], ref.at[me], ch)

    gather(1, gact_tok, "gact")

    arrived(lat_all.at[sib], "latsib")
    lat_half = lat_all[:, :, :, :, cols(c * 128, 128, 128)].reshape(384, 128)
    dlat_half = lat_all[:, :, :, :, cols(256 + c * 128, 128, 128)].reshape(384, 128)
    for d in (2, 1, 3, 0):
        b = ypeer(d)
        keep(d, 5, t_dot(dlat_half, DA[0, :, :, cols(b * 256, 256, 256)].reshape(384, 256)))
        keep(d, 6, t_dot(lat_half, gblock(b)))
        ship(d, "wb", part_b)

    for half_rows, n in ((first, 0), (second, 1)):
        arrived(A.at[2, half_rows], f"a2h{n}")
        arrived(A.at[1, half_rows], f"a1h{n}")
    dense(A.at[1], DA.at[1, c])
    dense(A.at[2], DA.at[2, c])
    remote(DA.at[1, c], DA.at[1, c], "asib1", seq=sib)
    remote(DA.at[2, c], DA.at[2, c], "asib2", seq=sib)
    A1, A2 = DA.at[1, c], DA.at[2, c]

    @pl.loop(0, 4)
    def _(b):
        here = cols(b * 256, 256, 256)
        o = (
            acc_o[:, here] + dot(A1[:, here], W[b, 3]) + dot(A2[:, here], W[b, 4])
            + dot(pair[:, 0:256], W[b, 6])
        )
        stage[0, :, :, :, here] = o.astype(BF).reshape(GROUPS, 3, 2, 256)

    gather(0, out_tok, "out")

    arrived(DA.at[1, sib], "asib1")
    arrived(DA.at[2, sib], "asib2")
    for d in (2, 1, 3, 0):
        b = ypeer(d)
        g = gblock(b)
        keep(d, 3, t_dot(half(1, b), g))
        keep(d, 4, t_dot(half(2, b), g))
        ship(d, "wc", part_c)

    for name, start, count in (("wa", 0, 3), ("wb", 5, 2), ("wc", 3, 2)):
        for d in range(1, 4):
            arrived(wg_recv.at[d - 1, pl.ds(start, count)], f"{name}{d}")
        for k in range(start, start + count):
            far_sum = wg_recv[0, k].astype(F32) + wg_recv[1, k].astype(F32)
            wg_out[k] = wg_out[k] + far_sum + wg_recv[2, k].astype(F32)
    arrived(stage.at[1], "gact")
    arrived(stage.at[0], "out")

    most = pl.ds(0, GROUPS - 1)
    top = pl.ds(0, 128)
    sent(G.at[0, most], "g")
    sent(A.at[0, most], "a")
    sent(W.at[0, 7, top], "zfar3")
    sent(W.at[0, 8, top], "zfar4")
    sent(W.at[0, far, top], "farsib")
    for d in range(1, 4):
        sent(W.at[0, low, top], f"low{d}")
        sent(W.at[0, low, top], f"lows{d}")
        sent(W.at[0, fly, top], f"fly{d}")
        sent(W.at[0, fly, top], f"flys{d}")
        sent(W.at[0, far, top], f"far{d}")
        sent(W.at[0, far, top], f"fars{d}")
        sent(latx, f"latx{d}")
        sent(latx, f"bcx{d}")
        sent(wg_send.at[d - 1, part_a], f"wa{d}")
        sent(wg_send.at[d - 1, part_b], f"wb{d}")
        sent(wg_send.at[d - 1, part_c], f"wc{d}")
    sent(G.at[0], "g1")
    sent(G.at[0], "g2")
    for ch in ("gsib", "asib0", "asib1", "asib2"):
        sent(DG.at[0], ch)
    for ch in ("a1h0", "a1h1", "a2h0", "a2h1"):
        sent(A.at[0, first], ch)
    sent(latx.at[pl.ds(0, 7)], "latz")
    sent(latx.at[pl.ds(0, 7)], "bcz")
    sent(lat_all.at[0], "latsib")
    sent(stage.at[0, most], "out")
    sent(stage.at[1, most], "gact")


def exchange(act, grad, bfly, low_u, low_v):
    tok = (GROUPS, 3, 2, 1024)
    any_space = pl.BlockSpec(memory_space=pl.ANY)
    vmem = pl.BlockSpec(memory_space=pltpu.VMEM)
    return pl.pallas_call(
        kernel,
        out_shape=(
            jax.ShapeDtypeStruct(tok, BF),
            jax.ShapeDtypeStruct(tok, BF),
            jax.ShapeDtypeStruct((7, 128, 256), F32),
        ),
        in_specs=[any_space] * 5,
        out_specs=(any_space, any_space, vmem),
        scratch_shapes=[
            pltpu.VMEM((3,) + tok, BF),
            pltpu.VMEM((3,) + tok, BF),
            pltpu.VMEM((3, 2, 192, 1024), BF),
            pltpu.VMEM((2, 192, 1024), BF),
            pltpu.VMEM((192, 1024), BF),
            pltpu.VMEM((192, 1024), BF),
            pltpu.VMEM((4, 9, 256, 256), BF),
            pltpu.VMEM((192, 1024), F32),
            pltpu.VMEM((192, 1024), F32),
            pltpu.VMEM((2,) + tok, BF),
            pltpu.VMEM((GROUPS, 3, 2, 512), BF),
            pltpu.VMEM((3, 8, 3, 2, 512), BF),
            pltpu.VMEM((8, 3, 2, 512), BF),
            pltpu.VMEM((8, 3, 2, 512), BF),
            pltpu.VMEM((3, 2, 512), BF),
            pltpu.VMEM((2, GROUPS, 3, 2, 512), BF),
            pltpu.VMEM((3, 7, 128, 256), BF),
            pltpu.VMEM((3, 7, 128, 256), BF),
            pltpu.SemaphoreType.DMA((len(CHANNELS),)),
            pltpu.SemaphoreType.DMA((len(CHANNELS),)),
        ],
        compiler_params=pltpu.CompilerParams(
            collective_id=0, has_side_effects=True, vmem_limit_bytes=48 * 2**20
        ),
    )(act, grad, bfly, low_u, low_v)


def gelu_tanh(value):
    return jax.nn.gelu(value, approximate=True)


def by_group(rows):
    return rows.reshape(3, 2, GROUPS, 1024).transpose(2, 0, 1, 3)


def by_token(groups):
    return groups.transpose(1, 2, 0, 3).reshape(6, 32768)


def on_device(pre_act, butterfly, low_u, low_v, grad_out):
    pre_f = pre_act.astype(F32)
    act_tok = gelu_tanh(pre_f).astype(BF)
    out_g, gact_g, wg = exchange(
        by_group(act_tok), by_group(grad_out), butterfly[0], low_u, low_v
    )
    unused, pullback = jax.vjp(gelu_tanh, pre_f)
    grad_pre = pullback(by_token(gact_g).astype(F32))[0].astype(BF)
    return by_token(out_g), grad_pre, wg[None, 0:5], wg[5].T, wg[6]


def solution(mesh):
    whole = Mesh(mesh.devices.reshape(4, 8, 4, 2), ("x", "z", "y", "seq"))
    hid = ("x", "z", "y")
    tokens = P(hid + ("seq",), None)
    return jax.shard_map(
        on_device,
        mesh=whole,
        in_specs=(tokens, P(hid, None, None, None), P(hid, None), P(None, hid), tokens),
        out_specs=(tokens, tokens, P(hid, None, "seq", None), P(hid, "seq"), P("seq", hid)),
        check_vma=False,
    )
```

time: 117 us -> 99.7 us (0.85)
  Pallas kernels: 105 us -> 87.5 us
    pallas_call x1, Pallas kernels: 105 us -> 87.5 us  [exchange(): pl.pallas_call(kernel, out_shape=(jax.ShapeDtypeStruct(tok, BF), jax.Shap...]
where the time goes in v3:
time: 99.7 us; the launch traced here: 98.5 us
  Pallas kernels  87.5 us (88%)
  local copies, waits for them, and re-layouts  7.05 us (7%)
  other arithmetic  3.21 us (3%)
    pallas_call x1, Pallas kernels, exchange(): pl.pallas_call(kernel, out_shape=(jax.ShapeDtypeStruct(tok, BF), jax.Shap...  87.5 us
    unnamed x15, local copies, waits for them, and re-layouts  4.35 us

profile of v3, /device:TPU:2, one launch (start us, length us, event | category | flops | bytes accessed | tf_op | source)
XLA Modules:
  0.0 98.5 jit_solution(17154079562017007311)
XLA Ops:
  0.6 1.4 %fusion.7 = bf16[6,32768]{1,0:T(8,128)(2,1)S(1)} fusion(bf16[6,32768]{1,0:T(8,128)(2,1)} %param.5), kind=kLoop, calls=%fused_computation.12 | loop fusion | flops 1966080 | bytes 786432 | tf_op jit(solution)/shard_map/convert_element_type | solution.py:409
  2.0 0.0 copy-start.4
  2.1 0.2 copy.16
  2.3 0.8 copy-done.4
  3.1 0.2 copy.17
  3.3 0.0 copy-start
  3.3 0.0 copy-start.1
  3.3 0.0 copy-start.2
  3.3 0.8 copy_bitcast_fusion
  4.2 0.2 copy-done
  4.4 0.0 copy-done.1
  4.4 0.0 copy-done.2
  4.5 87.5 %shard_map.92 = (bf16[32,3,2,1024]{3,2,1,0:T(2,128)(2,1)S(1)}, bf16[32,3,2,1024]{3,2,1,0:T(2,128)(2,1)S(1)}, f32[7,128,256]{2,1,0:T(8,128)S(1)}) custom-call(bf16[32,3,2,1024]{3,2,1,0:T(2,128)(2,1)S(1)} %get-tuple-element.24.act, bf16[32,3,2,1024]{3,2,1,0:T(2,128)(2,1)S(1)} %get-tuple-element.23.grad, bf16[5,256,256]{2,1,0:T(8,128)(2,1)S(1)} %bitcast.28, ...), custom_call_target="tpu_custom_call" | custom-call | tf_op jit(solution)/shard_map/pallas_call | solution.py:358
  92.0 0.7 slice_bitcast_fusion.1
  92.6 0.8 copy.15
  93.4 0.9 slice_bitcast_fusion
  94.3 0.3 convert_bitcast_fusion
  94.6 0.3 copy.14
  94.8 0.0 copy-start.3
  94.8 0.5 copy.19
  95.3 0.5 copy-done.3
  95.9 1.5 %fusion.3 = bf16[6,32768]{1,0:T(8,128)(2,1)} fusion(bf16[6,32768]{1,0:T(8,128)(2,1)S(1)} %copy-done.3, f32[6,32768]{1,0:T(8,128)S(1)} %bitcast.30), kind=kLoop, calls=%fused_computation.8 | loop fusion | flops 4128768 | bytes 1572864 | tf_op jit(solution)/shard_map/convert_element_type | solution.py:414
  97.4 0.1 copy.13
  97.5 1.0 %copy.18 = bf16[1,6,32,1024]{3,1,2,0:T(8,128)(2,1)} copy(bf16[1,6,32,1024]{3,2,1,0:T(8,128)(2,1)S(1)} %bitcast.35) | data formatting | bytes 786432
Async XLA Ops:
  2.0 1.0 %copy-start.4 = (bf16[6,32768]{1,0:T(8,128)(2,1)S(1)}, bf16[6,32768]{1,0:T(8,128)(2,1)}, u32[]{:S(2)}) copy-start(bf16[6,32768]{1,0:T(8,128)(2,1)} %param.9) | copy-start | bytes 1179652
  3.3 1.1 %copy-start = (bf16[1,5,256,256]{3,2,1,0:T(8,128)(2,1)S(1)}, bf16[1,5,256,256]{3,2,1,0:T(8,128)(2,1)}, u32[]{:S(2)}) copy-start(bf16[1,5,256,256]{3,2,1,0:T(8,128)(2,1)} %param.6) | copy-start | bytes 1966084
  3.3 1.1 %copy-start.1 = (bf16[256,256]{1,0:T(8,128)(2,1)S(1)}, bf16[256,256]{1,0:T(8,128)(2,1)}, u32[]{:S(2)}) copy-start(bf16[256,256]{1,0:T(8,128)(2,1)} %low_u.1) | copy-start | bytes 393220
  3.3 1.1 %copy-start.2 = (bf16[256,256]{1,0:T(8,128)(2,1)S(1)}, bf16[256,256]{1,0:T(8,128)(2,1)}, u32[]{:S(2)}) copy-start(bf16[256,256]{1,0:T(8,128)(2,1)} %low_v.1) | copy-start | bytes 393220
  94.8 1.0 %copy-start.3 = (bf16[6,32768]{1,0:T(8,128)(2,1)S(1)}, bf16[6,32768]{1,0:T(8,128)(2,1)}, u32[]{:S(2)}) copy-start(bf16[6,32768]{1,0:T(8,128)(2,1)} %param.5) | copy-start | bytes 1179652

commit v4 on v3

--- a/solution.py
+++ b/solution.py
@@ -37,7 +37,7 @@
 
 
 CHANNELS = (
-    "g", "a", "own", "zfar3", "zfar4", "g1", "g2", "gsib", "asib0", "asib1", "asib2", "farsib",
+    "pre", "gin", "g", "a", "own", "zfar3", "zfar4", "g1", "g2", "gsib", "asib0", "asib1", "asib2", "farsib",
     "latz", "bcz", "latsib", "out", "gact", "a1h0", "a1h1", "a2h0", "a2h1",
 ) + tuple(
     name + str(d)
@@ -47,9 +47,14 @@
 CH = {name: i for i, name in enumerate(CHANNELS)}
 
 
+def gelu_tanh(value):
+    return jax.nn.gelu(value, approximate=True)
+
+
 def kernel(
-    act, grad, bfly, low_u, low_v,
-    out_tok, gact_tok, wg_out,
+    pre_hbm, grad_hbm, bfly, low_u, low_v,
+    out_ref, gp_ref, gb_ref, gu_ref, gv_ref,
+    pre, grad_in, act, grad, out_tok, gact_tok, wg_own,
     A, G, DA, DG, DG1, DG2, W, acc_o, acc_g, stage, lat_send, latx_recv, latx, latz_recv,
     lat_own, lat_all, wg_send, wg_recv, send_sem, recv_sem,
 ):
@@ -87,6 +92,9 @@
     def xrows(xv):
         return pl.ds(xv * 8, 8)
 
+    local(pre_hbm, pre, "pre")
+    local(grad_hbm, grad_in, "gin")
+
     barrier = pltpu.get_barrier_semaphore()
 
     @pl.loop(1, GROUPS)
@@ -97,6 +105,14 @@
     for d in range(1, 4):
         pl.semaphore_signal(barrier, 1, device_id={"y": ypeer(d)}, device_id_type=MESH)
     pl.semaphore_signal(barrier, 1, device_id={"seq": sib}, device_id_type=MESH)
+
+    arrived(grad_in, "gin")
+
+    @pl.loop(0, GROUPS)
+    def _(q):
+        grad[q] = grad_in[:, cols(q * 1024, 1024, 1024)].reshape(3, 2, 1024)
+
+    arrived(pre, "pre")
     pl.semaphore_wait(barrier, GROUPS + 3)
 
     def scatter(src, dst, ch):
@@ -117,6 +133,12 @@
         remote(low_v.at[mine], W.at[y, 6, mine], f"low{d}", y=ypeer(d))
     remote(bfly.at[3, mine], W.at[y, 7, mine], "zfar3", z=z1)
     remote(bfly.at[4, mine], W.at[y, 8, mine], "zfar4", z=z2)
+
+    @pl.loop(0, GROUPS)
+    def _(q):
+        value = gelu_tanh(pre[:, cols(q * 1024, 1024, 1024)].astype(F32))
+        act[q] = value.astype(BF).reshape(3, 2, 1024)
+
     scatter(act, A.at[0], "a")
     for d in range(1, 4):
         remote(bfly.at[:, mine], W.at[y, fly, mine], f"fly{d}", y=ypeer(d))
@@ -212,7 +234,7 @@
 
     def keep(d, k, value):
         if d == 0:
-            wg_out[k] = value * FACTOR
+            wg_own[k] = value * FACTOR
         else:
             wg_send[d - 1, k] = (value * FACTOR).astype(BF)
 
@@ -310,14 +332,30 @@
         keep(d, 4, t_dot(half(2, b), g))
         ship(d, "wc", part_c)
 
-    for name, start, count in (("wa", 0, 3), ("wb", 5, 2), ("wc", 3, 2)):
+    arrived(stage.at[1], "gact")
+
+    @pl.loop(0, GROUPS)
+    def _(q):
+        here = cols(q * 1024, 1024, 1024)
+        slope = jax.vjp(gelu_tanh, pre[:, here].astype(F32))[1]
+        gp_ref[:, here] = slope(gact_tok[q].reshape(6, 1024).astype(F32))[0].astype(BF)
+
+    def total_of(k):
+        far_sum = wg_recv[0, k].astype(F32) + wg_recv[1, k].astype(F32)
+        return wg_own[k] + far_sum + wg_recv[2, k].astype(F32)
+
+    for name, rows in (("wa", part_a), ("wb", part_b), ("wc", part_c)):
         for d in range(1, 4):
-            arrived(wg_recv.at[d - 1, pl.ds(start, count)], f"{name}{d}")
-        for k in range(start, start + count):
-            far_sum = wg_recv[0, k].astype(F32) + wg_recv[1, k].astype(F32)
-            wg_out[k] = wg_out[k] + far_sum + wg_recv[2, k].astype(F32)
-    arrived(stage.at[1], "gact")
+            arrived(wg_recv.at[d - 1, rows], f"{name}{d}")
+    for k in range(5):
+        gb_ref[k] = total_of(k)
+    gu_ref[...] = total_of(5).T
+    gv_ref[...] = total_of(6)
     arrived(stage.at[0], "out")
+
+    @pl.loop(0, GROUPS)
+    def _(q):
+        out_ref[:, cols(q * 1024, 1024, 1024)] = out_tok[q].reshape(6, 1024)
 
     most = pl.ds(0, GROUPS - 1)
     top = pl.ds(0, 128)
@@ -351,20 +389,29 @@
     sent(stage.at[1, most], "gact")
 
 
-def exchange(act, grad, bfly, low_u, low_v):
+def exchange(pre_act, grad_out, bfly, low_u, low_v):
     tok = (GROUPS, 3, 2, 1024)
     any_space = pl.BlockSpec(memory_space=pl.ANY)
     vmem = pl.BlockSpec(memory_space=pltpu.VMEM)
     return pl.pallas_call(
         kernel,
         out_shape=(
-            jax.ShapeDtypeStruct(tok, BF),
-            jax.ShapeDtypeStruct(tok, BF),
-            jax.ShapeDtypeStruct((7, 128, 256), F32),
+            jax.ShapeDtypeStruct((6, 32768), BF),
+            jax.ShapeDtypeStruct((6, 32768), BF),
+            jax.ShapeDtypeStruct((5, 128, 256), F32),
+            jax.ShapeDtypeStruct((256, 128), F32),
+            jax.ShapeDtypeStruct((128, 256), F32),
         ),
         in_specs=[any_space] * 5,
-        out_specs=(any_space, any_space, vmem),
+        out_specs=(vmem,) * 5,
         scratch_shapes=[
+            pltpu.VMEM((6, 32768), BF),
+            pltpu.VMEM((6, 32768), BF),
+            pltpu.VMEM(tok, BF),
+            pltpu.VMEM(tok, BF),
+            pltpu.VMEM(tok, BF),
+            pltpu.VMEM(tok, BF),
+            pltpu.VMEM((7, 128, 256), F32),
             pltpu.VMEM((3,) + tok, BF),
             pltpu.VMEM((3,) + tok, BF),
             pltpu.VMEM((3, 2, 192, 1024), BF),
@@ -387,32 +434,38 @@
             pltpu.SemaphoreType.DMA((len(CHANNELS),)),
         ],
         compiler_params=pltpu.CompilerParams(
-            collective_id=0, has_side_effects=True, vmem_limit_bytes=48 * 2**20
+            collective_id=0, has_side_effects=True, vmem_limit_bytes=67043328
         ),
-    )(act, grad, bfly, low_u, low_v)
-
-
-def gelu_tanh(value):
-    return jax.nn.gelu(value, approximate=True)
-
-
-def by_group(rows):
-    return rows.reshape(3, 2, GROUPS, 1024).transpose(2, 0, 1, 3)
-
-
-def by_token(groups):
-    return groups.transpose(1, 2, 0, 3).reshape(6, 32768)
+    )(pre_act, grad_out, bfly, low_u, low_v)
+
+
+def store_kernel(*refs):
+    sources, targets, sem = refs[0:5], refs[5:10], refs[10]
+    copies = [
+        pltpu.make_async_copy(source, target, sem.at[i])
+        for i, (source, target) in enumerate(zip(sources, targets))
+    ]
+    for copy in copies:
+        copy.start()
+    for copy in copies:
+        copy.wait()
+
+
+def store(*values):
+    any_space = pl.BlockSpec(memory_space=pl.ANY)
+    return pl.pallas_call(
+        store_kernel,
+        out_shape=tuple(jax.ShapeDtypeStruct(v.shape, v.dtype) for v in values),
+        in_specs=[pl.BlockSpec(memory_space=pltpu.VMEM)] * 5,
+        out_specs=(any_space,) * 5,
+        scratch_shapes=[pltpu.SemaphoreType.DMA((5,))],
+    )(*values)
 
 
 def on_device(pre_act, butterfly, low_u, low_v, grad_out):
-    pre_f = pre_act.astype(F32)
-    act_tok = gelu_tanh(pre_f).astype(BF)
-    out_g, gact_g, wg = exchange(
-        by_group(act_tok), by_group(grad_out), butterfly[0], low_u, low_v
-    )
-    unused, pullback = jax.vjp(gelu_tanh, pre_f)
-    grad_pre = pullback(by_token(gact_g).astype(F32))[0].astype(BF)
-    return by_token(out_g), grad_pre, wg[None, 0:5], wg[5].T, wg[6]
+    parts = exchange(pre_act, grad_out, butterfly[0], low_u, low_v)
+    out, grad_pre, gb, gu, gv = parts
+    return out, grad_pre, gb[None], gu, gv
 
 
 def solution(mesh):

time: 99.7 us -> 97 us (0.973)
  other arithmetic: 3.21 us -> 0 us
  Pallas kernels: 87.5 us -> 89.3 us
  local copies, waits for them, and re-layouts: 7.05 us -> 5.83 us
    convert_element_type x3 -> x0, other arithmetic: 3.21 us -> none  [the longest x2 1.8 us: on_device(): grad_pre = pullback(by_token(gact_g).astype(F32))[0].astype(BF)]
    pallas_call x1, Pallas kernels: 87.5 us -> 89.3 us  [exchange(): pl.pallas_call(kernel, out_shape=(jax.ShapeDtypeStruct((6, 32768), BF), j...]
    unnamed x15 -> x13, local copies, waits for them, and re-layouts: 4.35 us -> 5.83 us
where the time goes in v4:
time: 97 us; the launch traced here: 95.8 us
  Pallas kernels  89.3 us (92%)
  local copies, waits for them, and re-layouts  5.83 us (6%)
    pallas_call x1, Pallas kernels, exchange(): pl.pallas_call(kernel, out_shape=(jax.ShapeDtypeStruct((6, 32768), BF), j...  89.3 us
    unnamed x13, local copies, waits for them, and re-layouts  5.83 us

profile of v4, /device:TPU:2, one launch (start us, length us, event | category | flops | bytes accessed | tf_op | source)
XLA Modules:
  0.0 95.8 jit_solution(2682840981951213152)
XLA Ops:
  0.6 89.3 %shard_map.92 = (bf16[6,32768]{1,0:T(8,128)(2,1)}, bf16[6,32768]{1,0:T(8,128)(2,1)}, f32[5,128,256]{2,1,0:T(8,128)}, f32[256,128]{1,0:T(8,128)}, f32[128,256]{1,0:T(8,128)}) custom-call(bf16[6,32768]{1,0:T(8,128)(2,1)} %pre_hbm.1, bf16[6,32768]{1,0:T(8,128)(2,1)} %grad_hbm.1, bf16[5,256,256]{2,1,0:T(8,128)(2,1)} %bitcast.3, bf16[256,256]{1,0:T(8,128)(2,1)} %low_u.1, ...), custom_call_target="tpu_custom_call" | custom-call | tf_op jit(solution)/shard_map/pallas_call | solution.py:396
  89.9 0.0 copy-start.1
  89.9 1.9 %copy.15 = bf16[6,32768]{1,0:T(8,128)(2,1)} copy(bf16[6,32768]{1,0:T(8,128)(2,1)} %get-tuple-element.20) | data formatting | bytes 786432
  91.9 0.0 copy-done.1
  91.9 0.0 copy-start
  91.9 0.8 copy.16
  92.7 0.5 copy-done
  93.2 0.0 copy-start.3
  93.2 0.8 copy.17
  94.0 0.2 copy-done.3
  94.2 0.0 copy-start.2
  94.2 0.7 copy.18
  94.8 0.3 copy-done.2
  95.1 0.7 copy.19
Async XLA Ops:
  89.9 1.9 %copy-start.1 = (bf16[6,32768]{1,0:T(8,128)(2,1)S(1)}, bf16[6,32768]{1,0:T(8,128)(2,1)}, u32[]{:S(2)}) copy-start(bf16[6,32768]{1,0:T(8,128)(2,1)} %get-tuple-element.21) | copy-start | bytes 1179652
  91.9 1.3 %copy-start = (f32[5,128,256]{2,1,0:T(8,128)S(1)}, f32[5,128,256]{2,1,0:T(8,128)}, u32[]{:S(2)}) copy-start(f32[5,128,256]{2,1,0:T(8,128)} %get-tuple-element.12) | copy-start | bytes 1966084
  93.2 1.0 %copy-start.3 = (f32[256,128]{1,0:T(8,128)S(1)}, f32[256,128]{1,0:T(8,128)}, u32[]{:S(2)}) copy-start(f32[256,128]{1,0:T(8,128)} %get-tuple-element.23) | copy-start | bytes 393220
  94.2 1.0 copy-start.2

commit v5 on v4

--- a/solution.py
+++ b/solution.py
@@ -434,9 +434,9 @@
             pltpu.SemaphoreType.DMA((len(CHANNELS),)),
         ],
         compiler_params=pltpu.CompilerParams(
-            collective_id=0, has_side_effects=True, vmem_limit_bytes=67043328
+            collective_id=0, has_side_effects=True, vmem_limit_bytes=48 * 2**20
         ),
-    )(pre_act, grad_out, bfly, low_u, low_v)
+    )(*(pltpu.with_memory_space_constraint(v, pltpu.HBM) for v in (pre_act, grad_out, bfly, low_u, low_v)))
 
 
 def store_kernel(*refs):

time: 97 us -> 93.5 us (0.964)
  local copies, waits for them, and re-layouts: 5.83 us -> 3.73 us
  Pallas kernels: 89.3 us -> 88 us
    unnamed x13 -> x5, local copies, waits for them, and re-layouts: 5.83 us -> 3.73 us
    pallas_call x1, Pallas kernels: 89.3 us -> 88 us  [exchange(): pl.pallas_call(kernel, out_shape=(jax.ShapeDtypeStruct((6, 32768), BF), j...]
where the time goes in v5:
time: 93.5 us; the launch traced here: 92.4 us
  Pallas kernels  88 us (94%)
  local copies, waits for them, and re-layouts  3.73 us (4%)
    pallas_call x1, Pallas kernels, exchange(): pl.pallas_call(kernel, out_shape=(jax.ShapeDtypeStruct((6, 32768), BF), j...  88 us
    unnamed x5, local copies, waits for them, and re-layouts  3.73 us

profile of v5, /device:TPU:2, one launch (start us, length us, event | category | flops | bytes accessed | tf_op | source)
XLA Modules:
  0.0 92.4 jit_solution(3929652975975250988)
XLA Ops:
  0.6 88.0 %shard_map.92 = (bf16[6,32768]{1,0:T(8,128)(2,1)S(1)}, bf16[6,32768]{1,0:T(8,128)(2,1)S(1)}, f32[5,128,256]{2,1,0:T(8,128)S(1)}, f32[256,128]{1,0:T(8,128)S(1)}, f32[128,256]{1,0:T(8,128)S(1)}) custom-call(bf16[6,32768]{1,0:T(8,128)(2,1)} %pre_hbm.1, bf16[6,32768]{1,0:T(8,128)(2,1)} %grad_hbm.1, bf16[5,256,256]{2,1,0:T(8,128)(2,1)} %bitcast.3, ...), custom_call_target="tpu_custom_call" | custom-call | tf_op jit(solution)/shard_map/pallas_call | solution.py:396
  88.7 0.8 copy.15
  89.5 0.8 copy.16
  90.2 0.8 copy.17
  91.1 0.7 copy.18
  91.7 0.7 copy.19

commit v6 on v5

--- a/solution.py
+++ b/solution.py
@@ -108,7 +108,7 @@
 
     arrived(grad_in, "gin")
 
-    @pl.loop(0, GROUPS)
+    @pl.loop(0, GROUPS, unroll=4)
     def _(q):
         grad[q] = grad_in[:, cols(q * 1024, 1024, 1024)].reshape(3, 2, 1024)
 
@@ -134,7 +134,7 @@
     remote(bfly.at[3, mine], W.at[y, 7, mine], "zfar3", z=z1)
     remote(bfly.at[4, mine], W.at[y, 8, mine], "zfar4", z=z2)
 
-    @pl.loop(0, GROUPS)
+    @pl.loop(0, GROUPS, unroll=4)
     def _(q):
         value = gelu_tanh(pre[:, cols(q * 1024, 1024, 1024)].astype(F32))
         act[q] = value.astype(BF).reshape(3, 2, 1024)
@@ -334,7 +334,7 @@
 
     arrived(stage.at[1], "gact")
 
-    @pl.loop(0, GROUPS)
+    @pl.loop(0, GROUPS, unroll=4)
     def _(q):
         here = cols(q * 1024, 1024, 1024)
         slope = jax.vjp(gelu_tanh, pre[:, here].astype(F32))[1]
@@ -353,7 +353,7 @@
     gv_ref[...] = total_of(6)
     arrived(stage.at[0], "out")
 
-    @pl.loop(0, GROUPS)
+    @pl.loop(0, GROUPS, unroll=4)
     def _(q):
         out_ref[:, cols(q * 1024, 1024, 1024)] = out_tok[q].reshape(6, 1024)
 

time: 93.5 us -> 93.4 us (level)
  no operation moved by 1% of the time
where the time goes in v6:
time: 93.4 us; the launch traced here: 92.3 us
  Pallas kernels  87.9 us (94%)
  local copies, waits for them, and re-layouts  3.73 us (4%)
    pallas_call x1, Pallas kernels, exchange(): pl.pallas_call(kernel, out_shape=(jax.ShapeDtypeStruct((6, 32768), BF), j...  87.9 us
    unnamed x5, local copies, waits for them, and re-layouts  3.73 us

profile of v6, /device:TPU:2, one launch (start us, length us, event | category | flops | bytes accessed | tf_op | source)
XLA Modules:
  0.0 92.3 jit_solution(10355857540263415113)
XLA Ops:
  0.6 87.9 %shard_map.92 = (bf16[6,32768]{1,0:T(8,128)(2,1)S(1)}, bf16[6,32768]{1,0:T(8,128)(2,1)S(1)}, f32[5,128,256]{2,1,0:T(8,128)S(1)}, f32[256,128]{1,0:T(8,128)S(1)}, f32[128,256]{1,0:T(8,128)S(1)}) custom-call(bf16[6,32768]{1,0:T(8,128)(2,1)} %pre_hbm.1, bf16[6,32768]{1,0:T(8,128)(2,1)} %grad_hbm.1, bf16[5,256,256]{2,1,0:T(8,128)(2,1)} %bitcast.3, ...), custom_call_target="tpu_custom_call" | custom-call | tf_op jit(solution)/shard_map/pallas_call | solution.py:396
  88.5 0.8 copy.15
  89.3 0.8 copy.16
  90.1 0.8 copy.17
  91.0 0.7 copy.18
  91.6 0.7 copy.19
